TPU v7x, 32 devices: a whole 2x2x4 slice. The times are simulated.
32 devices in a mesh: row: 2 (over y), col: 8 (over z, x), depth: 2 (over core).
Axes of the slice: x: 2, y: 2, z: 4, core: 2. Of those that a mesh axis runs over, the one named last changes fastest.
Arguments:
- a_tiles: bfloat16 [2, 16, 8, 2, 128, 128], P('row', ('col', 'depth')), may hold values from -1.5 to 1.5
- a_cols: int32 [2, 16, 8, 2], P('row', ('col', 'depth')), may hold values from 0 to 15, as said below
- a_count: int32 [2, 16, 8], P('row', ('col', 'depth')), may hold values from 0 to 2, as said below
- b_tiles: bfloat16 [4, 2, 2, 8, 16, 1, 128, 128], P(None, 'row', 'depth', 'col'), may hold values from -1.5 to 1.5
- b_cols: int32 [4, 2, 2, 8, 16, 1], P(None, 'row', 'depth', 'col'), may hold values from 0 to 11, as said below
- b_count: int32 [4, 2, 2, 8, 16], P(None, 'row', 'depth', 'col'), may hold values from 0 to 1, as said below
Outputs:
- product: bfloat16 [2048, 12288], P(('row', 'depth'), 'col')
Inputs may be any that keep to these rules, and one draw needn't show every extreme that they name: The entries of a_cols for one row group, inner panel and block row are distinct. `a_count`: some block row holds 2 blocks in every draw. The entries of b_cols for one inner block row are distinct. `b_count`: some inner block row holds 1 block in every draw.
All inputs are finite; a program needn't handle non-finite values.
Results may differ from a plain program's by a relative error of at most 0.001.
Values may be sent and summed in bfloat16 or wider, within the bound.
A program may use at most 128 MiB of HBM per device.

v0:
```python
import functools
import math

import jax
import jax.numpy as jnp
from jax import lax
from jax.experimental import pallas as pl
from jax.experimental.pallas import tpu as pltpu
from jax.sharding import PartitionSpec as P

BC = 12
SHIFTS = 4


def for_sending(array):
    return jax.tree.map(lambda a: a.astype(jnp.bfloat16) if a.dtype == jnp.float32 else a, array)


def shifted(value, axis, steps):
    count = lax.axis_size(axis)
    pairs = [(source, (source + steps) % count) for source in range(count)]
    return lax.ppermute(value, axis, pairs)


def dense_panel(tiles_b, cols_b, count_b, width):
    slot_ids = lax.broadcasted_iota(jnp.int32, cols_b.shape, 1)
    valid_slot = slot_ids < count_b[:, None]
    targets = lax.broadcasted_iota(jnp.int32, (1, 1, width), 2)
    placing = jnp.logical_and(cols_b[:, :, None] == targets, valid_slot[:, :, None]).astype(
        jnp.bfloat16
    )
    spread = jnp.einsum("kuc,kuab->kacb", placing, tiles_b, preferred_element_type=jnp.float32)
    inner_blocks = tiles_b.shape[0]
    tile_size = tiles_b.shape[2]
    return spread.astype(jnp.bfloat16).reshape(inner_blocks, tile_size, width * tile_size)


def panel_product(tiles_a, cols_a, count_a, rows_dense):
    block_rows = tiles_a.shape[0]
    per_row = tiles_a.shape[1]
    tile_size = tiles_a.shape[2]
    slot_ids = lax.broadcasted_iota(jnp.int32, cols_a.shape, 1)
    valid_slot = slot_ids < count_a[:, None]
    masked = jnp.where(valid_slot[:, :, None, None], tiles_a, jnp.zeros_like(tiles_a))
    group_rows = math.gcd(block_rows, 4)

    def one_group(pieces):
        tiles_part, cols_part = pieces
        chosen = jnp.take(rows_dense, cols_part, axis=0)
        return jnp.einsum("rtab,rtbn->ran", tiles_part, chosen, preferred_element_type=jnp.float32)

    grouped = lax.map(
        one_group,
        (
            masked.reshape(block_rows // group_rows, group_rows, per_row, tile_size, tile_size),
            cols_a.reshape(block_rows // group_rows, group_rows, per_row),
        ),
    )
    return grouped.reshape(block_rows, tile_size, rows_dense.shape[2])


def roll_slots(stack, offset):
    slot_total = stack[0].shape[0]
    return tuple(
        (
            lax.dynamic_slice_in_dim(
                jnp.concatenate([member, member], 0), offset % slot_total, slot_total, 0
            )
            for member in stack
        )
    )


def select_if(flag, fresh, stale):
    return tuple((jnp.where(flag, new_part, old_part) for new_part, old_part in zip(fresh, stale)))


def local(a_tiles, a_cols, a_count, b_tiles, b_cols, b_count):
    rows_axis = lax.axis_size("row")
    cols_axis = lax.axis_size("col")
    row_group = lax.axis_index("row")
    col_group = lax.axis_index("col")
    tiles_a = a_tiles[0, 0]
    cols_a = a_cols[0, 0]
    count_a = a_count[0, 0]
    tiles_b = b_tiles[:, 0, 0, 0]
    cols_b = b_cols[:, 0, 0, 0]
    count_b = b_count[:, 0, 0, 0]
    for bit_pos in range((rows_axis - 1).bit_length()):
        stride = 1 << bit_pos
        moved = (
            shifted(tiles_a, "col", cols_axis - stride),
            shifted(for_sending(cols_a), "col", cols_axis - stride).astype(cols_a.dtype),
            shifted(for_sending(count_a), "col", cols_axis - stride).astype(count_a.dtype),
        )
        tiles_a, cols_a, count_a = select_if(
            row_group // stride % 2 == 1, moved, (tiles_a, cols_a, count_a)
        )
    for bit_pos in range((cols_axis - 1).bit_length()):
        stride = 1 << bit_pos
        nearby = stride % rows_axis
        if nearby:
            moved = (
                shifted(tiles_b, "row", rows_axis - nearby),
                shifted(for_sending(cols_b), "row", rows_axis - nearby).astype(cols_b.dtype),
                shifted(for_sending(count_b), "row", rows_axis - nearby).astype(count_b.dtype),
            )
        else:
            moved = (tiles_b, cols_b, count_b)
        moved = roll_slots(moved, (row_group + stride) // rows_axis)
        tiles_b, cols_b, count_b = select_if(
            col_group // stride % 2 == 1, moved, (tiles_b, cols_b, count_b)
        )
    tile_size = tiles_a.shape[2]
    running = jnp.zeros((tiles_a.shape[0], tile_size, BC * tile_size), jnp.float32)
    for turn_no in range(SHIFTS):
        current_tiles = tiles_b[0]
        current_cols = cols_b[0]
        current_count = count_b[0]
        rows_dense = dense_panel(current_tiles, current_cols, current_count, BC)
        running = running + panel_product(tiles_a, cols_a, count_a, rows_dense)
        if turn_no + 1 < SHIFTS:
            tiles_a, cols_a, count_a = (
                shifted(tiles_a, "col", cols_axis - 1),
                shifted(for_sending(cols_a), "col", cols_axis - 1).astype(cols_a.dtype),
                shifted(for_sending(count_a), "col", cols_axis - 1).astype(count_a.dtype),
            )
            moved = (
                shifted(tiles_b, "row", rows_axis - 1),
                shifted(for_sending(cols_b), "row", rows_axis - 1).astype(cols_b.dtype),
                shifted(for_sending(count_b), "row", rows_axis - 1).astype(count_b.dtype),
            )
            tiles_b, cols_b, count_b = roll_slots(moved, (row_group + 1) // rows_axis)
    flat_running = running.reshape(-1, running.shape[2])
    summed = lax.psum(flat_running, "depth")
    half_rows = flat_running.shape[0] // lax.axis_size("depth")
    own_rows = lax.dynamic_slice_in_dim(summed, lax.axis_index("depth") * half_rows, half_rows, 0)
    return own_rows.astype(jnp.bfloat16)


REACH = SHIFTS + 1
CHUNKS = 4
WIDTH = 1
MESH_ID = pl.DeviceIdType.MESH


def gather_multiply(n_col, a_cols, a_count, b_cols, b_count, a_ref, b_ref, out_ref, A, Bn0, Bn1, Bf0, Bf1,
                    Gn0, Gn1, Gf0, Gf1, MA, MC, MB, MK, SA, SC, SB, SK, run, ktab, ptab, ltab,
                    send_m, recv_m, send_a, recv_a, send_b, recv_b, local_sem):
    row = lax.axis_index("row")
    col = lax.axis_index("col")
    dep = lax.axis_index("depth")
    side = lax.rem(col, 2)
    half = A.shape[2]
    per_row = A.shape[3]
    size = A.shape[4]
    inner = Bn0.shape[0]
    out_cols = out_ref.shape[1] // size
    terms = SHIFTS * 2 * per_row
    zero_at = half * terms
    parts = half // WIDTH
    units = [(d, pl.ds(h * WIDTH, WIDTH)) for d in range(2) for h in range(parts)]
    count_u = len(units)
    step_b = inner // CHUNKS

    def at(col_offset, flip_depth=False, flip_row=False):
        return (
            1 - row if flip_row else row,
            lax.rem(col + col_offset + n_col, n_col),
            1 - dep if flip_depth else dep,
        )

    chain_dev = at(-2)
    twin_dev = at(0, True)
    row_dev = at(0, False, True)
    side_dev = (row, col + 1 - 2 * side, dep)

    def remote(src, dst, ssem, rsem, dev):
        return pltpu.make_async_remote_copy(
            src_ref=src, dst_ref=dst, send_sem=ssem, recv_sem=rsem, device_id=dev, device_id_type=MESH_ID
        )

    s_near = [side + 2 * k for k in range(2)]
    s_far = [1 - side + 2 * k for k in range(2)]
    m_near = [lax.rem(row + col + s, n_col) // 2 for s in s_near]
    m_far = [lax.rem(1 - row + col + s, n_col) // 2 for s in s_far]
    m_mine = [lax.rem(row + col + s, n_col) // 2 for s in s_far]
    near_own, near_twin = (Bn0, Bn1), (Gn0, Gn1)
    far_own, far_twin = (Bf0, Bf1), (Gf0, Gf1)
    index_local = [
        pltpu.make_async_copy(src, dst.at[0], local_sem.at[n])
        for n, (src, dst) in enumerate(((a_cols, MA), (a_count, MC), (b_cols, MB), (b_count, MK)))
    ]
    b_local = [pltpu.make_async_copy(b_ref.at[m_near[k]], near_own[k], local_sem.at[4 + k]) for k in range(2)]
    a_local = pltpu.make_async_copy(a_ref.at[pl.ds(dep * half, half)], A.at[0, 0], local_sem.at[6])
    for copy in index_local + b_local + [a_local]:
        copy.start()

    barrier = pltpu.get_barrier_semaphore()
    reach = REACH - 1
    offsets = [o for o in range(1, n_col) if o <= reach or n_col - o <= reach]
    peers = [at(o, flip) for o in offsets for flip in (False, True)]
    peers += [twin_dev, row_dev, at(0, True, True)]
    for peer in peers:
        pl.semaphore_signal(barrier, inc=1, device_id=peer, device_id_type=MESH_ID)
    pl.semaphore_wait(barrier, len(peers))

    index_copies = []
    for q in range(REACH):
        for d in range(2):
            slot = q * 2 + d
            if slot:
                for n, (src, dst) in enumerate(((a_cols, MA), (a_count, MC))):
                    index_copies.append(
                        remote(src, dst.at[slot], send_m.at[n, slot], recv_m.at[n, slot], at(-q, d == 1))
                    )
    for slot in range(1, 4):
        for n, (src, dst) in enumerate(((b_cols, MB), (b_count, MK))):
            index_copies.append(
                remote(
                    src, dst.at[slot], send_m.at[2 + n, slot], recv_m.at[2 + n, slot],
                    at(0, slot % 2 == 1, slot >= 2),
                )
            )

    swap = [
        remote(
            a_ref.at[pl.ds((1 - dep) * half + h * WIDTH, WIDTH)], A.at[0, 1, pl.ds(h * WIDTH, WIDTH)],
            send_a.at[0, h], recv_a.at[0, parts + h], twin_dev,
        )
        for h in range(parts)
    ]
    first = [a_ref.at[pl.ds(dep * half + h * WIDTH, WIDTH)] for h in range(parts)]
    first += [A.at[0, 1, pl.ds(h * WIDTH, WIDTH)] for h in range(parts)]

    def to_panel(p, sources, send_row, dev):
        return [
            remote(src, A.at[p, d, r], send_a.at[send_row, u], recv_a.at[p, u], dev)
            for u, ((d, r), src) in enumerate(zip(units, sources))
        ]

    def panel(p):
        return [A.at[p, d, r] for d, r in units]

    chain = to_panel(2, first, 1, chain_dev)
    chain2 = to_panel(4, panel(2), 2, chain_dev)
    odd1 = to_panel(1, first, 3, side_dev)
    odd3 = to_panel(3, panel(2), 4, side_dev)
    even1 = to_panel(1, panel(2), 3, side_dev)
    even3 = to_panel(3, panel(4), 4, side_dev)

    near_b = [
        remote(b_ref.at[m_near[k]], near_twin[k], send_b.at[2 * k, CHUNKS], recv_b.at[2 * k, CHUNKS], twin_dev)
        for k in range(2)
    ]
    far_b, pass_b = [], []
    for k in range(2):
        for c in range(CHUNKS):
            part = pl.ds(c * step_b, step_b)
            far_b.append(
                remote(
                    b_ref.at[m_far[k], part], far_own[k].at[part],
                    send_b.at[2 * k, c], recv_b.at[2 * k, c], row_dev,
                )
            )
            pass_b.append(
                remote(
                    far_own[k].at[part], far_twin[k].at[part],
                    send_b.at[2 * k + 1, c], recv_b.at[2 * k + 1, c], twin_dev,
                )
            )

    for copy in index_copies[:2] + index_copies[-6:]:
        copy.start()
    for copy in index_copies[2:-6]:
        copy.start()
    for r in range(parts):
        chain[r].start()
        swap[r].start()

        @pl.when(side == 1)
        def _():
            odd1[r].start()

    for copy in far_b:
        copy.start()
    for copy in near_b:
        copy.start()
    run[zero_at] = jnp.zeros(run.shape[1:], jnp.float32)
    for r in range(parts):
        swap[r].wait_recv()
        chain[parts + r].start()

        @pl.when(side == 1)
        def _():
            odd1[parts + r].start()

    groups = [(s, m, k, d, far) for k in range(2) for far, s, m in ((0, s_near[k], m_near[k]), (1, s_far[k], m_mine[k]))
              for d in range(2)]

    def tables(r, carry):
        cs = []
        for s, m, _, d, far in groups:
            slot = (s + row) * 2 + d
            used = SC[slot, 0, dep * half + r]
            for t in range(per_row):
                k = SA[slot, t, dep * half + r]
                c = SB[2 * far + d, m, 0, k]
                ok = jnp.logical_and(used > t, SK[2 * far + d, m, 0, k] > 0)
                c = jnp.where(ok, c, -1)
                here = r * terms + len(cs)
                before = jnp.int32(zero_at)
                for at_p, c_p in enumerate(cs):
                    before = jnp.where(c_p == c, r * terms + at_p, before)
                ktab[here] = k
                ptab[here] = before
                cs.append(c)
        for c in range(out_cols):
            last = jnp.int32(zero_at)
            for at_p, c_p in enumerate(cs):
                last = jnp.where(c_p == c, r * terms + at_p, last)
            ltab[r * out_cols + c] = last
        return carry

    def product(g, d, r, t, right):
        here = r * terms + g * per_row + t
        value = jnp.dot(A[groups[g][0] + row, d, r, t], right[ktab[here]], preferred_element_type=jnp.float32)
        run[here] = value + run[ptab[here]]

    def whole_group(g, right):
        d = groups[g][3]

        def one(t, carry):
            for r in range(half):
                product(g, d, r, t, right)
            return carry

        lax.fori_loop(0, per_row, one, 0)

    begin = count_u // 4
    lag = begin + count_u * 3 // 8
    for u in range(count_u):
        chain[u].wait_recv()
        chain2[u].start()

        @pl.when(side == 0)
        def _():
            even1[u].start()

        @pl.when(side == 1)
        def _():
            odd3[u].start()

        for c in range(u * CHUNKS // count_u, (u + 1) * CHUNKS // count_u):
            far_b[c].wait_recv()
            pass_b[c].start()
        if u == begin:
            for copy in index_local:
                copy.wait()
            for copy in index_copies:
                copy.wait_recv()
            scalars = [
                pltpu.make_async_copy(src, dst, local_sem.at[n])
                for n, (src, dst) in enumerate(((MA, SA), (MC, SC), (MB, SB), (MK, SK)))
            ]
            for copy in scalars:
                copy.start()
            for copy in scalars:
                copy.wait()
        for r in range(half):
            if u == begin + r * count_u // (2 * half):
                tables(r, 0)

    def near_unit(u):
        odd3[u].wait_recv()
        d, h = u // parts, u % parts
        for t in range(per_row):
            for r in range(h * WIDTH, (h + 1) * WIDTH):
                product(4 + d, d, r, t, (Bn1, Gn1)[d])

    done = 0
    for u in range(count_u):
        chain2[u].wait_recv()

        @pl.when(side == 0)
        def _():
            even3[u].start()

        for c in range(CHUNKS + u * CHUNKS // count_u, CHUNKS + (u + 1) * CHUNKS // count_u):
            far_b[c].wait_recv()
            pass_b[c].start()
        if u == begin:
            a_local.wait()
            for copy in b_local:
                copy.wait()
            for copy in near_b:
                copy.wait_recv()
            for copy in odd1:
                copy.wait_recv()
            for c in range(CHUNKS):
                pass_b[c].wait_recv()
        for g, right in enumerate((Bn0, Gn0, Bf0, Gf0)):
            if u == begin + g * count_u // 8:
                whole_group(g, right)
        if u >= lag:
            near_unit(done)
            done += 1
    for u in range(done, count_u):
        near_unit(u)
    whole_group(6, Bf1)
    for c in range(CHUNKS):
        pass_b[CHUNKS + c].wait_recv()
    whole_group(7, Gf1)

    def place(r, carry):
        rows = pl.ds(pl.multiple_of(r * size, size), size)
        for c in range(out_cols):
            out_ref[rows, c * size : (c + 1) * size] = run[ltab[r * out_cols + c]].astype(out_ref.dtype)
        return carry

    lax.fori_loop(0, half, place, 0)

    for copy in index_copies + swap + chain + chain2 + odd1 + odd3 + far_b + near_b + pass_b:
        copy.wait_send()


def local_fast(n_col, a_tiles, a_cols, a_count, b_tiles, b_cols, b_count):
    block_rows, per_row, size = a_tiles.shape[2:5]
    slots, inner = b_tiles.shape[0], b_tiles.shape[4]
    half = block_rows // 2
    terms = SHIFTS * 2 * per_row
    count = half * terms
    panels = REACH * 2
    hbm = pl.BlockSpec(memory_space=pltpu.HBM)
    vmem = pl.BlockSpec(memory_space=pltpu.VMEM)
    index_shapes = [(panels, per_row, block_rows), (panels, 1, block_rows), (4, slots, 1, inner), (4, slots, 1, inner)]
    right = pltpu.VMEM((inner, size, size), jnp.bfloat16)
    call = pl.pallas_call(
        functools.partial(gather_multiply, n_col),
        out_shape=jax.ShapeDtypeStruct((half * size, BC * size), jnp.bfloat16),
        in_specs=[hbm] * 6,
        out_specs=vmem,
        scratch_shapes=[pltpu.VMEM((REACH, 2, half, per_row, size, size), jnp.bfloat16)]
        + [right] * 8
        + [pltpu.VMEM(shape, jnp.int32) for shape in index_shapes]
        + [pltpu.SMEM(shape, jnp.int32) for shape in index_shapes]
        + [
            pltpu.VMEM((count + 1, size, size), jnp.float32),
            pltpu.SMEM((count,), jnp.int32),
            pltpu.SMEM((count,), jnp.int32),
            pltpu.SMEM((half * BC,), jnp.int32),
            pltpu.SemaphoreType.DMA((4, panels)),
            pltpu.SemaphoreType.DMA((4, panels)),
            pltpu.SemaphoreType.DMA((5, 2 * half)),
            pltpu.SemaphoreType.DMA((REACH, 2 * half)),
            pltpu.SemaphoreType.DMA((4, CHUNKS + 1)),
            pltpu.SemaphoreType.DMA((4, CHUNKS + 1)),
            pltpu.SemaphoreType.DMA((7,)),
        ],
        compiler_params=pltpu.CompilerParams(
            collective_id=0, has_side_effects=True, vmem_limit_bytes=40 * 1024 * 1024
        ),
    )
    operands = [
        jnp.swapaxes(a_cols.reshape(block_rows, per_row), 0, 1),
        a_count.reshape(1, block_rows),
        b_cols.reshape(slots, 1, inner),
        b_count.reshape(slots, 1, inner),
        a_tiles.reshape(block_rows, per_row, size, size),
        b_tiles.reshape(slots, inner, size, size),
    ]
    return call(*(pltpu.with_memory_space_constraint(x, pltpu.HBM) for x in operands))


def solution(mesh):
    placed = (
        P("row", ("col", "depth"), None, None, None, None),
        P("row", ("col", "depth"), None, None),
        P("row", ("col", "depth"), None),
        P(None, "row", "depth", "col", None, None, None, None),
        P(None, "row", "depth", "col", None, None),
        P(None, "row", "depth", "col", None),
    )
    n_col = mesh.shape["col"]
    if mesh.shape["row"] == 2 and mesh.shape["depth"] == 2 and n_col % 2 == 0 and n_col > SHIFTS:
        body = functools.partial(local_fast, n_col)
    else:
        body = local
    return jax.shard_map(
        body, mesh=mesh, in_specs=placed, out_specs=P(("row", "depth"), "col"), check_vma=False
    )
```

profile of v0, /device:TPU:30, one launch (start us, length us, event | category | flops | bytes accessed | tf_op | source)
XLA Modules:
  0.0 36.3 jit_solution(6725883281973962387)
XLA Ops:
  0.0 35.1 %shard_map.64 = bf16[512,1536]{1,0:T(8,128)(2,1)S(1)} custom-call(s32[2,8]{1,0:T(2,128)} %bitcast.16, s32[1,8]{1,0:T(1,128)} %bitcast.17, s32[4,1,16]{2,1,0:T(1,128)} %bitcast.14, s32[4,1,16]{2,1,0:T(1,128)} %bitcast.15, bf16[8,2,128,128]{3,2,1,0:T(8,128)(2,1)} %bitcast.13, bf16[4,16,128,128]{3,2,1,0:T(8,128)(2,1)} %bitcast.12), custom_call_target="tpu_custom_call" | custom-call | tf_op jit(solution)/shard_map/pallas_call | solution.py:472
  35.1 1.1 %copy.10 = bf16[512,1536]{1,0:T(8,128)(2,1)} copy(bf16[512,1536]{1,0:T(8,128)(2,1)S(1)} %shard_map.64) | data formatting | bytes 3145728
where the time goes:
time: 36.7 us; the launch traced here: 36.3 us
  Pallas kernels  35.1 us (96%)
  local copies, waits for them, and re-layouts  1.15 us (3%)
    pallas_call x1, Pallas kernels, local_fast(): call(*(pltpu.with_memory_space_constraint(x, pltpu.HBM) for x in operands))  35.1 us
    unnamed x1, local copies, waits for them, and re-layouts  1.15 us

commit v1 on v0

--- a/solution.py
+++ b/solution.py
@@ -46,7 +46,10 @@
 
     def one_group(pieces):
         tiles_part, cols_part = pieces
-        chosen = jnp.take(rows_dense, cols_part, axis=0)
+        picks = lax.broadcasted_iota(jnp.int32, cols_part.shape + (rows_dense.shape[0],), 2)
+        picks = (cols_part[:, :, None] == picks).astype(rows_dense.dtype)
+        chosen = jnp.einsum("rtk,kbn->rtbn", picks, rows_dense, preferred_element_type=jnp.float32)
+        chosen = chosen.astype(rows_dense.dtype)
         return jnp.einsum("rtab,rtbn->ran", tiles_part, chosen, preferred_element_type=jnp.float32)
 
     grouped = lax.map(
@@ -144,9 +147,8 @@
 MESH_ID = pl.DeviceIdType.MESH
 
 
-def gather_multiply(n_col, a_cols, a_count, b_cols, b_count, a_ref, b_ref, out_ref, A, Bn0, Bn1, Bf0, Bf1,
-                    Gn0, Gn1, Gf0, Gf1, MA, MC, MB, MK, SA, SC, SB, SK, run, ktab, ptab, ltab,
-                    send_m, recv_m, send_a, recv_a, send_b, recv_b, local_sem):
+def gather_multiply(n_col, a_cols, a_count, b_cols, b_count, a_ref, b_ref, out_ref, A, Bn0, Bn1, Gn0, Gn1, Bf0, Bf1, Gf0, Gf1, MA, MC, MB, MK, SA, SC, SB, SK, run, ktab, ptab, ltab,
+                    send_m, recv_m, send_a, recv_a, send_b, recv_b, recv_n, recv_p, local_sem):
     row = lax.axis_index("row")
     col = lax.axis_index("col")
     dep = lax.axis_index("depth")
@@ -180,6 +182,9 @@
             src_ref=src, dst_ref=dst, send_sem=ssem, recv_sem=rsem, device_id=dev, device_id_type=MESH_ID
         )
 
+    def drain(ref, sem):
+        pltpu.make_async_copy(ref, ref, sem).wait()
+
     s_near = [side + 2 * k for k in range(2)]
     s_far = [1 - side + 2 * k for k in range(2)]
     m_near = [lax.rem(row + col + s, n_col) // 2 for s in s_near]
@@ -212,13 +217,13 @@
             if slot:
                 for n, (src, dst) in enumerate(((a_cols, MA), (a_count, MC))):
                     index_copies.append(
-                        remote(src, dst.at[slot], send_m.at[n, slot], recv_m.at[n, slot], at(-q, d == 1))
+                        remote(src, dst.at[slot], send_m.at[n], recv_m.at[n], at(-q, d == 1))
                     )
     for slot in range(1, 4):
         for n, (src, dst) in enumerate(((b_cols, MB), (b_count, MK))):
             index_copies.append(
                 remote(
-                    src, dst.at[slot], send_m.at[2 + n, slot], recv_m.at[2 + n, slot],
+                    src, dst.at[slot], send_m.at[2 + n], recv_m.at[2 + n],
                     at(0, slot % 2 == 1, slot >= 2),
                 )
             )
@@ -226,7 +231,7 @@
     swap = [
         remote(
             a_ref.at[pl.ds((1 - dep) * half + h * WIDTH, WIDTH)], A.at[0, 1, pl.ds(h * WIDTH, WIDTH)],
-            send_a.at[0, h], recv_a.at[0, parts + h], twin_dev,
+            send_a.at[0], recv_a.at[0, parts + h], twin_dev,
         )
         for h in range(parts)
     ]
@@ -235,7 +240,7 @@
 
     def to_panel(p, sources, send_row, dev):
         return [
-            remote(src, A.at[p, d, r], send_a.at[send_row, u], recv_a.at[p, u], dev)
+            remote(src, A.at[p, d, r], send_a.at[send_row], recv_a.at[p, u], dev)
             for u, ((d, r), src) in enumerate(zip(units, sources))
         ]
 
@@ -250,7 +255,7 @@
     even3 = to_panel(3, panel(4), 4, side_dev)
 
     near_b = [
-        remote(b_ref.at[m_near[k]], near_twin[k], send_b.at[2 * k, CHUNKS], recv_b.at[2 * k, CHUNKS], twin_dev)
+        remote(b_ref.at[m_near[k]], near_twin[k], send_b.at[0], recv_n, twin_dev)
         for k in range(2)
     ]
     far_b, pass_b = [], []
@@ -260,13 +265,13 @@
             far_b.append(
                 remote(
                     b_ref.at[m_far[k], part], far_own[k].at[part],
-                    send_b.at[2 * k, c], recv_b.at[2 * k, c], row_dev,
+                    send_b.at[1], recv_b.at[k, c], row_dev,
                 )
             )
             pass_b.append(
                 remote(
                     far_own[k].at[part], far_twin[k].at[part],
-                    send_b.at[2 * k + 1, c], recv_b.at[2 * k + 1, c], twin_dev,
+                    send_b.at[2], recv_p.at[k], twin_dev,
                 )
             )
 
@@ -357,8 +362,8 @@
         if u == begin:
             for copy in index_local:
                 copy.wait()
-            for copy in index_copies:
-                copy.wait_recv()
+            for n, ref in enumerate((MA, MC, MB, MK)):
+                drain(ref.at[pl.ds(1, ref.shape[0] - 1)], recv_m.at[n])
             scalars = [
                 pltpu.make_async_copy(src, dst, local_sem.at[n])
                 for n, (src, dst) in enumerate(((MA, SA), (MC, SC), (MB, SB), (MK, SK)))
@@ -393,12 +398,10 @@
             a_local.wait()
             for copy in b_local:
                 copy.wait()
-            for copy in near_b:
-                copy.wait_recv()
+            drain(A.at[pl.ds(0, 2)], recv_n)
             for copy in odd1:
                 copy.wait_recv()
-            for c in range(CHUNKS):
-                pass_b[c].wait_recv()
+            drain(Gf0, recv_p.at[0])
         for g, right in enumerate((Bn0, Gn0, Bf0, Gf0)):
             if u == begin + g * count_u // 8:
                 whole_group(g, right)
@@ -408,8 +411,7 @@
     for u in range(done, count_u):
         near_unit(u)
     whole_group(6, Bf1)
-    for c in range(CHUNKS):
-        pass_b[CHUNKS + c].wait_recv()
+    drain(Gf1, recv_p.at[1])
     whole_group(7, Gf1)
 
     def place(r, carry):
@@ -420,8 +422,13 @@
 
     lax.fori_loop(0, half, place, 0)
 
-    for copy in index_copies + swap + chain + chain2 + odd1 + odd3 + far_b + near_b + pass_b:
-        copy.wait_send()
+    for n, ref in enumerate((MA, MC, MB, MK)):
+        drain(ref.at[pl.ds(0, ref.shape[0] - 1)], send_m.at[n])
+    drain(A.at[0, 1], send_a.at[0])
+    for n in range(1, 5):
+        drain(A.at[n], send_a.at[n])
+    for n in range(3):
+        drain(A.at[pl.ds(0, 2)], send_b.at[n])
 
 
 def local_fast(n_col, a_tiles, a_cols, a_count, b_tiles, b_cols, b_count):
@@ -434,14 +441,13 @@
     hbm = pl.BlockSpec(memory_space=pltpu.HBM)
     vmem = pl.BlockSpec(memory_space=pltpu.VMEM)
     index_shapes = [(panels, per_row, block_rows), (panels, 1, block_rows), (4, slots, 1, inner), (4, slots, 1, inner)]
-    right = pltpu.VMEM((inner, size, size), jnp.bfloat16)
     call = pl.pallas_call(
         functools.partial(gather_multiply, n_col),
         out_shape=jax.ShapeDtypeStruct((half * size, BC * size), jnp.bfloat16),
         in_specs=[hbm] * 6,
         out_specs=vmem,
         scratch_shapes=[pltpu.VMEM((REACH, 2, half, per_row, size, size), jnp.bfloat16)]
-        + [right] * 8
+        + [pltpu.VMEM((inner, size, size), jnp.bfloat16)] * 8
         + [pltpu.VMEM(shape, jnp.int32) for shape in index_shapes]
         + [pltpu.SMEM(shape, jnp.int32) for shape in index_shapes]
         + [
@@ -449,12 +455,14 @@
             pltpu.SMEM((count,), jnp.int32),
             pltpu.SMEM((count,), jnp.int32),
             pltpu.SMEM((half * BC,), jnp.int32),
-            pltpu.SemaphoreType.DMA((4, panels)),
-            pltpu.SemaphoreType.DMA((4, panels)),
-            pltpu.SemaphoreType.DMA((5, 2 * half)),
+            pltpu.SemaphoreType.DMA((4,)),
+            pltpu.SemaphoreType.DMA((4,)),
+            pltpu.SemaphoreType.DMA((5,)),
             pltpu.SemaphoreType.DMA((REACH, 2 * half)),
-            pltpu.SemaphoreType.DMA((4, CHUNKS + 1)),
-            pltpu.SemaphoreType.DMA((4, CHUNKS + 1)),
+            pltpu.SemaphoreType.DMA((3,)),
+            pltpu.SemaphoreType.DMA((2, CHUNKS)),
+            pltpu.SemaphoreType.DMA,
+            pltpu.SemaphoreType.DMA((2,)),
             pltpu.SemaphoreType.DMA((7,)),
         ],
         compiler_params=pltpu.CompilerParams(

time: 36.7 us -> 35.4 us (0.965)
  Pallas kernels: 35.1 us -> 33.8 us
    pallas_call x1, Pallas kernels: 35.1 us -> 33.8 us  [local_fast(): call(*(pltpu.with_memory_space_constraint(x, pltpu.HBM) for x in operands))]
where the time goes in v1:
time: 35.4 us; the launch traced here: 35 us
  Pallas kernels  33.8 us (95%)
  local copies, waits for them, and re-layouts  1.15 us (3%)
    pallas_call x1, Pallas kernels, local_fast(): call(*(pltpu.with_memory_space_constraint(x, pltpu.HBM) for x in operands))  33.8 us
    unnamed x1, local copies, waits for them, and re-layouts  1.15 us

profile of v1, /device:TPU:30, one launch (start us, length us, event | category | flops | bytes accessed | tf_op | source)
XLA Modules:
  0.0 35.0 jit_solution(9031722585295778823)
XLA Ops:
  0.0 33.8 %shard_map.64 = bf16[512,1536]{1,0:T(8,128)(2,1)S(1)} custom-call(s32[2,8]{1,0:T(2,128)} %bitcast.16, s32[1,8]{1,0:T(1,128)} %bitcast.17, s32[4,1,16]{2,1,0:T(1,128)} %bitcast.14, s32[4,1,16]{2,1,0:T(1,128)} %bitcast.15, bf16[8,2,128,128]{3,2,1,0:T(8,128)(2,1)} %bitcast.13, bf16[4,16,128,128]{3,2,1,0:T(8,128)(2,1)} %bitcast.12), custom_call_target="tpu_custom_call" | custom-call | tf_op jit(solution)/shard_map/pallas_call | solution.py:480
  33.8 1.1 %copy.10 = bf16[512,1536]{1,0:T(8,128)(2,1)} copy(bf16[512,1536]{1,0:T(8,128)(2,1)S(1)} %shard_map.64) | data formatting | bytes 3145728

commit v2 on v1

v2 whole, which is shorter than its diff:
```python
import functools
import math

import jax
import jax.numpy as jnp
from jax import lax
from jax.experimental import pallas as pl
from jax.experimental.pallas import tpu as pltpu
from jax.sharding import PartitionSpec as P

BC = 12
SHIFTS = 4


def for_sending(array):
    return jax.tree.map(lambda a: a.astype(jnp.bfloat16) if a.dtype == jnp.float32 else a, array)


def shifted(value, axis, steps):
    count = lax.axis_size(axis)
    pairs = [(source, (source + steps) % count) for source in range(count)]
    return lax.ppermute(value, axis, pairs)


def dense_panel(tiles_b, cols_b, count_b, width):
    slot_ids = lax.broadcasted_iota(jnp.int32, cols_b.shape, 1)
    valid_slot = slot_ids < count_b[:, None]
    targets = lax.broadcasted_iota(jnp.int32, (1, 1, width), 2)
    placing = jnp.logical_and(cols_b[:, :, None] == targets, valid_slot[:, :, None]).astype(
        jnp.bfloat16
    )
    spread = jnp.einsum("kuc,kuab->kacb", placing, tiles_b, preferred_element_type=jnp.float32)
    inner_blocks = tiles_b.shape[0]
    tile_size = tiles_b.shape[2]
    return spread.astype(jnp.bfloat16).reshape(inner_blocks, tile_size, width * tile_size)


def panel_product(tiles_a, cols_a, count_a, rows_dense):
    block_rows = tiles_a.shape[0]
    per_row = tiles_a.shape[1]
    tile_size = tiles_a.shape[2]
    slot_ids = lax.broadcasted_iota(jnp.int32, cols_a.shape, 1)
    valid_slot = slot_ids < count_a[:, None]
    masked = jnp.where(valid_slot[:, :, None, None], tiles_a, jnp.zeros_like(tiles_a))
    group_rows = math.gcd(block_rows, 4)

    def one_group(pieces):
        tiles_part, cols_part = pieces
        picks = lax.broadcasted_iota(jnp.int32, cols_part.shape + (rows_dense.shape[0],), 2)
        picks = (cols_part[:, :, None] == picks).astype(rows_dense.dtype)
        chosen = jnp.einsum("rtk,kbn->rtbn", picks, rows_dense, preferred_element_type=jnp.float32)
        chosen = chosen.astype(rows_dense.dtype)
        return jnp.einsum("rtab,rtbn->ran", tiles_part, chosen, preferred_element_type=jnp.float32)

    grouped = lax.map(
        one_group,
        (
            masked.reshape(block_rows // group_rows, group_rows, per_row, tile_size, tile_size),
            cols_a.reshape(block_rows // group_rows, group_rows, per_row),
        ),
    )
    return grouped.reshape(block_rows, tile_size, rows_dense.shape[2])


def roll_slots(stack, offset):
    slot_total = stack[0].shape[0]
    return tuple(
        (
            lax.dynamic_slice_in_dim(
                jnp.concatenate([member, member], 0), offset % slot_total, slot_total, 0
            )
            for member in stack
        )
    )


def select_if(flag, fresh, stale):
    return tuple((jnp.where(flag, new_part, old_part) for new_part, old_part in zip(fresh, stale)))


def local(a_tiles, a_cols, a_count, b_tiles, b_cols, b_count):
    rows_axis = lax.axis_size("row")
    cols_axis = lax.axis_size("col")
    row_group = lax.axis_index("row")
    col_group = lax.axis_index("col")
    tiles_a = a_tiles[0, 0]
    cols_a = a_cols[0, 0]
    count_a = a_count[0, 0]
    tiles_b = b_tiles[:, 0, 0, 0]
    cols_b = b_cols[:, 0, 0, 0]
    count_b = b_count[:, 0, 0, 0]
    for bit_pos in range((rows_axis - 1).bit_length()):
        stride = 1 << bit_pos
        moved = (
            shifted(tiles_a, "col", cols_axis - stride),
            shifted(for_sending(cols_a), "col", cols_axis - stride).astype(cols_a.dtype),
            shifted(for_sending(count_a), "col", cols_axis - stride).astype(count_a.dtype),
        )
        tiles_a, cols_a, count_a = select_if(
            row_group // stride % 2 == 1, moved, (tiles_a, cols_a, count_a)
        )
    for bit_pos in range((cols_axis - 1).bit_length()):
        stride = 1 << bit_pos
        nearby = stride % rows_axis
        if nearby:
            moved = (
                shifted(tiles_b, "row", rows_axis - nearby),
                shifted(for_sending(cols_b), "row", rows_axis - nearby).astype(cols_b.dtype),
                shifted(for_sending(count_b), "row", rows_axis - nearby).astype(count_b.dtype),
            )
        else:
            moved = (tiles_b, cols_b, count_b)
        moved = roll_slots(moved, (row_group + stride) // rows_axis)
        tiles_b, cols_b, count_b = select_if(
            col_group // stride % 2 == 1, moved, (tiles_b, cols_b, count_b)
        )
    tile_size = tiles_a.shape[2]
    running = jnp.zeros((tiles_a.shape[0], tile_size, BC * tile_size), jnp.float32)
    for turn_no in range(SHIFTS):
        current_tiles = tiles_b[0]
        current_cols = cols_b[0]
        current_count = count_b[0]
        rows_dense = dense_panel(current_tiles, current_cols, current_count, BC)
        running = running + panel_product(tiles_a, cols_a, count_a, rows_dense)
        if turn_no + 1 < SHIFTS:
            tiles_a, cols_a, count_a = (
                shifted(tiles_a, "col", cols_axis - 1),
                shifted(for_sending(cols_a), "col", cols_axis - 1).astype(cols_a.dtype),
                shifted(for_sending(count_a), "col", cols_axis - 1).astype(count_a.dtype),
            )
            moved = (
                shifted(tiles_b, "row", rows_axis - 1),
                shifted(for_sending(cols_b), "row", rows_axis - 1).astype(cols_b.dtype),
                shifted(for_sending(count_b), "row", rows_axis - 1).astype(count_b.dtype),
            )
            tiles_b, cols_b, count_b = roll_slots(moved, (row_group + 1) // rows_axis)
    flat_running = running.reshape(-1, running.shape[2])
    summed = lax.psum(flat_running, "depth")
    half_rows = flat_running.shape[0] // lax.axis_size("depth")
    own_rows = lax.dynamic_slice_in_dim(summed, lax.axis_index("depth") * half_rows, half_rows, 0)
    return own_rows.astype(jnp.bfloat16)


REACH = SHIFTS + 1
CHUNKS = 4
LATE = 1
MESH_ID = pl.DeviceIdType.MESH


def gather_multiply(n_col, a_cols, a_count, b_cols, b_count, a_ref, b_ref, out_ref, A, Bn0, Bn1, Bf0, Bf1,
                    Gn0, Gn1, Gf0, Gf1, MA, MB, SA, SB, run, ktab, ptab, ltab,
                    send_m, recv_m, send_a, recv_a, send_b, recv_b, recv_n, ready, local_sem):
    row = lax.axis_index("row")
    col = lax.axis_index("col")
    dep = lax.axis_index("depth")
    side = lax.rem(col, 2)
    z = lax.div(col, 2)
    top = n_col // 2 - 1
    per_row, size = A.shape[1:3]
    units = A.shape[0] // REACH
    half = units // 2
    inner = Bn0.shape[0]
    out_cols = out_ref.shape[1] // size
    terms = SHIFTS * 2 * per_row
    zero_at = half * terms
    step_b = inner // CHUNKS
    row0, row1, side0, side1 = row == 0, row == 1, side == 0, side == 1

    def both(*flags):
        return functools.reduce(jnp.logical_and, flags)

    def at(col_offset, flip_depth=False, flip_row=False):
        return (
            1 - row if flip_row else row,
            lax.rem(col + col_offset + n_col, n_col),
            1 - dep if flip_depth else dep,
        )

    twin_dev, row_dev = at(0, True), at(0, False, True)
    side_dev = (row, col + 1 - 2 * side, dep)
    down, up, down2, up2 = at(-2), at(2), at(-4), at(4)

    def remote(src, dst, ssem, rsem, dev):
        return pltpu.make_async_remote_copy(
            src_ref=src, dst_ref=dst, send_sem=ssem, recv_sem=rsem, device_id=dev, device_id_type=MESH_ID
        )

    def signal(sem, dev):
        pl.semaphore_signal(sem, inc=1, device_id=dev, device_id_type=MESH_ID)

    def drain(ref, sem):
        pltpu.make_async_copy(ref, ref, sem).wait()

    def start(copies, *flags):
        def go():
            for copy in copies:
                copy.start()

        if flags:
            pl.when(both(*flags))(go)
        else:
            go()

    s_near = [side + 2 * k for k in range(2)]
    s_far = [1 - side + 2 * k for k in range(2)]
    m_near = [lax.rem(row + col + s, n_col) // 2 for s in s_near]
    m_far = [lax.rem(1 - row + col + s, n_col) // 2 for s in s_far]
    m_mine = [lax.rem(row + col + s, n_col) // 2 for s in s_far]
    near_own, near_twin = (Bn0, Bn1), (Gn0, Gn1)
    far_own, far_twin = (Bf0, Bf1), (Gf0, Gf1)

    index_local = [
        pltpu.make_async_copy(src, dst, local_sem.at[n])
        for n, (src, dst) in enumerate((
            (a_cols, MA.at[0, pl.ds(0, per_row)]), (a_count, MA.at[0, pl.ds(per_row, 1)]),
            (b_cols, MB.at[0, 0]), (b_count, MB.at[0, 1]),
        ))
    ]
    b_local = [pltpu.make_async_copy(b_ref.at[m_near[k]], near_own[k], local_sem.at[4 + k]) for k in range(2)]
    a_local = pltpu.make_async_copy(a_ref.at[pl.ds(dep * half, half)], A.at[pl.ds(0, half)], local_sem.at[6])
    start(index_local + b_local + [a_local])

    @pl.when(row0)
    def _():
        for slot in range(2 * SHIFTS, 2 * REACH):
            MA[slot] = jnp.zeros(MA.shape[1:], MA.dtype)

    barrier = pltpu.get_barrier_semaphore()
    signal(barrier, twin_dev)
    pl.when(row0)(lambda: signal(barrier, row_dev))
    pl.when(side0)(lambda: signal(barrier, side_dev))
    pl.when(z < top)(lambda: signal(barrier, up))
    pl.when(z == 0)(lambda: signal(barrier, down))
    pl.when(both(row1, z == 1))(lambda: signal(barrier, down2))
    greeted = 1 + row + side + jnp.where(z > 0, 1, 0) + jnp.where(z == top, 1 + row, 0)
    pl.semaphore_wait(barrier, greeted)
    pl.when(row1)(lambda: signal(ready.at[0], row_dev))
    pl.when(side1)(lambda: signal(ready.at[1], side_dev))
    pl.when(z == top)(lambda: signal(ready.at[2], up))
    pl.when(both(row1, z == top))(lambda: signal(ready.at[2], up2))

    def unit(p, u):
        return A.at[p * units + u]

    own = [a_ref.at[dep * half + r] for r in range(half)] + [unit(0, half + r) for r in range(half)]

    def to_panel(p, sources, n, dev):
        return [remote(src, unit(p, u), send_a.at[n], recv_a.at[p, u], dev) for u, src in enumerate(sources)]

    def panel(p):
        return [unit(p, u) for u in range(units)]

    swap = [
        remote(a_ref.at[(1 - dep) * half + r], unit(0, half + r), send_a.at[0], recv_a.at[0, r], twin_dev)
        for r in range(half)
    ]
    chain = to_panel(2, own, 1, down)
    chain2 = to_panel(4, panel(2), 2, down)
    skip = to_panel(4, own, 3, down2)
    own_x1 = to_panel(1, own, 4, side_dev)
    fwd_x1 = to_panel(1, panel(2), 4, side_dev)
    fwd_x3 = to_panel(3, panel(2), 5, side_dev)
    top_x3 = to_panel(3, panel(4), 5, side_dev)
    low_x3 = to_panel(3, panel(1), 6, down)
    late = range(units - LATE, units)

    near_b = [remote(b_ref.at[m_near[k]], near_twin[k], send_b.at[0], recv_n, twin_dev) for k in range(2)]
    far_b, pass_b = [], []
    for k in range(2):
        for c in range(CHUNKS):
            part = pl.ds(c * step_b, step_b)
            far_b.append(
                remote(b_ref.at[m_far[k], part], far_own[k].at[part], send_b.at[1], recv_b.at[k, c], row_dev)
            )
            pass_b.append(
                remote(
                    far_own[k].at[part], far_twin[k].at[part], send_b.at[2], recv_b.at[2 + k, 0], twin_dev
                )
            )

    def index_a(src, dst, n, sem, dev):
        return remote(MA.at[pl.ds(src, n)], MA.at[pl.ds(dst, n)], send_m.at[sem], recv_m.at[dst // 2], dev)

    swap_m = remote(MA.at[0], MA.at[1], send_m.at[0], recv_m.at[0], twin_dev)
    near_m = remote(MB.at[0], MB.at[1], send_m.at[1], recv_m.at[5], twin_dev)
    far_m = remote(MB.at[0], MB.at[2], send_m.at[1], recv_m.at[6], row_dev)
    pass_m = remote(MB.at[2], MB.at[3], send_m.at[1], recv_m.at[7], twin_dev)
    chain_m, chain2_m, skip_m = index_a(0, 4, 2, 0, down), index_a(4, 8, 2, 2, down), index_a(0, 8, 2, 3, down2)
    own_x1_m, fwd_x1_m = index_a(0, 2, 2, 0, side_dev), index_a(4, 2, 2, 0, side_dev)
    fwd_x3_m, low_x3_m = index_a(4, 6, 2, 4, side_dev), index_a(2, 6, 2, 4, down)

    for copy in index_local:
        copy.wait()
    start([swap_m] + swap)
    first = half // 2
    start(chain[:first], z > 0)
    start(own_x1[:first], side1)
    pl.when(row0)(lambda: pl.semaphore_wait(ready.at[0], 1))
    start([far_m] + far_b + [near_m] + near_b)
    swap_m.wait_recv()
    start([chain_m], z > 0)
    start([own_x1_m], side1)
    start(chain[first:half], z > 0)
    start(own_x1[first:half], side1)
    for r in range(half):
        swap[r].wait_recv()
    start(chain[half:], z > 0)
    start(own_x1[half:], side1)

    @pl.when(z == 0)
    def _():
        pl.semaphore_wait(ready.at[2], 1)
        start(chain[:first] + [chain_m] + chain[first:])

    @pl.when(both(row1, z == 1))
    def _():
        pl.semaphore_wait(ready.at[2], 1)
        start(skip[:1] + [skip_m])

    pl.when(side0)(lambda: pl.semaphore_wait(ready.at[1], 1))
    run[zero_at] = jnp.zeros(run.shape[1:], jnp.float32)

    def far_part(n):
        far_b[n].wait_recv()
        pass_b[n].start()

    def low(u):
        recv(1, u)
        start([low_x3[u]], side1, *([] if u in late else [row0]))

    def recv(p, u):
        drain(unit(p, u), recv_a.at[p, u])

    groups = [(s, m, k, d, far) for k in range(2) for far, s, m in ((0, s_near[k], m_near[k]), (1, s_far[k], m_mine[k]))
              for d in range(2)]

    def tables(r):
        cs = []
        for s, m, _, d, far in groups:
            slot = (s + row) * 2 + d
            used = SA[slot, per_row, dep * half + r]
            for t in range(per_row):
                k = SA[slot, t, dep * half + r]
                c = SB[2 * far + d, 0, m, 0, k]
                ok = jnp.logical_and(used > t, SB[2 * far + d, 1, m, 0, k] > 0)
                c = jnp.where(ok, c, -1)
                here = r * terms + len(cs)
                before = jnp.int32(zero_at)
                for at_p, c_p in enumerate(cs):
                    before = jnp.where(c_p == c, r * terms + at_p, before)
                ktab[here] = k
                ptab[here] = before
                cs.append(c)
        for c in range(out_cols):
            last = jnp.int32(zero_at)
            for at_p, c_p in enumerate(cs):
                last = jnp.where(c_p == c, r * terms + at_p, last)
            ltab[r * out_cols + c] = last

    def product(g, r, t, right):
        s, _, _, d, _ = groups[g]
        here = r * terms + g * per_row + t
        left = A[(s + row) * units + d * half + r, t]
        value = jnp.dot(left, right[ktab[here]], preferred_element_type=jnp.float32)
        run[here] = value + run[ptab[here]]

    def whole_group(g, right):
        def one(t, carry):
            for r in range(half):
                product(g, r, t, right)
            return carry

        lax.fori_loop(0, per_row, one, 0)

    def unit_of(g, r, right):
        for t in range(per_row):
            product(g, r, t, right)

    for u in range(units):
        recv(2, u)
        start([chain2[u]], row1, z > 0)
        start([fwd_x1[u]], side0)
        start([fwd_x3[u]], side1)
        if u == 0:
            drain(MA.at[pl.ds(4, 2)], recv_m.at[2])
            start([chain2_m], row1, z > 0)
            start([fwd_x1_m], side0)
            start([fwd_x3_m], side1)
            far_m.wait_recv()
            pass_m.start()
        if u == units - 2:
            start(skip[1:], row1, z == 1)
        if u == units // 2:
            drain(MA.at[pl.ds(2, 2)], recv_m.at[1])
            start([low_x3_m], side1)
        if u >= 3:
            low(u - 3)
        if u % 2:
            far_part(u // 2)

    def near_unit(u):
        pl.when(row != side)(lambda: recv(3, u))
        pl.when(both(row1, side1))(lambda: recv(4, u))
        unit_of(4 + u // half, u % half, (Bn1, Gn1)[u // half])

    near_done = 0
    for u in range(units):
        @pl.when(both(row1, side0))
        def _():
            recv(4, u)
            if u not in late:
                top_x3[u].start()

        if u < 3:
            low(units - 3 + u)
        if u == 0:
            drain(MA.at[pl.ds(6, 2)], recv_m.at[3])
            pl.when(row1)(lambda: drain(MA.at[pl.ds(8, 2)], recv_m.at[4]))
            near_m.wait_recv()
            pass_m.wait_recv()
            scalars = [pltpu.make_async_copy(MA, SA, local_sem.at[0]), pltpu.make_async_copy(MB, SB, local_sem.at[1])]
            start(scalars)
            for copy in scalars:
                copy.wait()
            for copy in b_local + [a_local]:
                copy.wait()
            drain(A.at[pl.ds(0, 2 * units)], recv_n)
            drain(A.at[pl.ds(0, units)], recv_b.at[2, 0])
        if u % 2:
            far_part(CHUNKS + u // 2)
        if 1 <= u <= half:
            tables(u - 1)
        if u == half:
            whole_group(0, Bn0)
        if u == half + 1:
            whole_group(1, Gn0)
            whole_group(2, Bf0)
        if u == half + 2:
            whole_group(3, Gf0)
        if u > half + 1:
            for w in range(near_done, near_done + 3):
                near_unit(w)
            near_done += 3
    for u in range(near_done, units):
        near_unit(u)

    def far_unit(u, right):
        pl.when(row == side)(lambda: recv(3, u))
        unit_of(6 + u // half, u % half, right)

    for u in range(half):
        far_unit(u, Bf1)
    drain(A.at[pl.ds(0, units)], recv_b.at[3, 0])
    for u in range(half, units):
        far_unit(u, Gf1)

    def place(r, carry):
        rows = pl.ds(pl.multiple_of(r * size, size), size)
        for c in range(out_cols):
            out_ref[rows, c * size : (c + 1) * size] = run[ltab[r * out_cols + c]].astype(out_ref.dtype)
        return carry

    lax.fori_loop(0, half, place, 0)

    def sent(n, sem, *flags):
        if flags:
            pl.when(both(*flags))(lambda: drain(A.at[pl.ds(0, n)], sem))
        else:
            drain(A.at[pl.ds(0, n)], sem)

    sent(half, send_a.at[0])
    sent(units, send_a.at[1])
    sent(units, send_a.at[2], row1, z > 0)
    sent(units, send_a.at[3], row1, z == 1)
    sent(units, send_a.at[4])
    sent(units, send_a.at[5], side1)
    sent(units - LATE, send_a.at[5], side0, row1)
    sent(units, send_a.at[6], side1, row0)
    sent(LATE, send_a.at[6], side1, row1)
    for n in range(3):
        sent(2 * units, send_b.at[n])
    drain(MA.at[pl.ds(0, 5)], send_m.at[0])
    drain(MB.at[pl.ds(0, 3)], send_m.at[1])
    pl.when(both(row1, z > 0))(lambda: drain(MA.at[pl.ds(0, 2)], send_m.at[2]))
    pl.when(both(row1, z == 1))(lambda: drain(MA.at[pl.ds(0, 2)], send_m.at[3]))
    pl.when(side1)(lambda: drain(MA.at[pl.ds(0, 4)], send_m.at[4]))


def local_fast(n_col, a_tiles, a_cols, a_count, b_tiles, b_cols, b_count):
    block_rows, per_row, size = a_tiles.shape[2:5]
    slots, inner = b_tiles.shape[0], b_tiles.shape[4]
    half = block_rows // 2
    count = half * SHIFTS * 2 * per_row
    hbm = pl.BlockSpec(memory_space=pltpu.HBM)
    index_shapes = [(REACH * 2, per_row + 1, block_rows), (4, 2, slots, 1, inner)]
    call = pl.pallas_call(
        functools.partial(gather_multiply, n_col),
        out_shape=jax.ShapeDtypeStruct((half * size, BC * size), jnp.bfloat16),
        in_specs=[hbm] * 6,
        out_specs=pl.BlockSpec(memory_space=pltpu.VMEM),
        scratch_shapes=[pltpu.VMEM((REACH * block_rows, per_row, size, size), jnp.bfloat16)]
        + [pltpu.VMEM((inner, size, size), jnp.bfloat16)] * 8
        + [pltpu.VMEM(shape, jnp.int32) for shape in index_shapes]
        + [pltpu.SMEM(shape, jnp.int32) for shape in index_shapes]
        + [
            pltpu.VMEM((count + 1, size, size), jnp.float32),
            pltpu.SMEM((count,), jnp.int32),
            pltpu.SMEM((count,), jnp.int32),
            pltpu.SMEM((half * BC,), jnp.int32),
            pltpu.SemaphoreType.DMA((5,)),
            pltpu.SemaphoreType.DMA((8,)),
            pltpu.SemaphoreType.DMA((7,)),
            pltpu.SemaphoreType.DMA((REACH, block_rows)),
            pltpu.SemaphoreType.DMA((3,)),
            pltpu.SemaphoreType.DMA((4, CHUNKS)),
            pltpu.SemaphoreType.DMA,
            pltpu.SemaphoreType.REGULAR((3,)),
            pltpu.SemaphoreType.DMA((7,)),
        ],
        compiler_params=pltpu.CompilerParams(
            collective_id=0, has_side_effects=True, vmem_limit_bytes=40 * 1024 * 1024
        ),
    )
    operands = [
        jnp.swapaxes(a_cols.reshape(block_rows, per_row), 0, 1),
        a_count.reshape(1, block_rows),
        b_cols.reshape(slots, 1, inner),
        b_count.reshape(slots, 1, inner),
        a_tiles.reshape(block_rows, per_row, size, size),
        b_tiles.reshape(slots, inner, size, size),
    ]
    return call(*(pltpu.with_memory_space_constraint(x, pltpu.HBM) for x in operands))


def solution(mesh):
    placed = (
        P("row", ("col", "depth"), None, None, None, None),
        P("row", ("col", "depth"), None, None),
        P("row", ("col", "depth"), None),
        P(None, "row", "depth", "col", None, None, None, None),
        P(None, "row", "depth", "col", None, None),
        P(None, "row", "depth", "col", None),
    )
    n_col = mesh.shape["col"]
    if mesh.shape["row"] == 2 and mesh.shape["depth"] == 2 and n_col == 2 * SHIFTS:
        body = functools.partial(local_fast, n_col)
    else:
        body = local
    return jax.shard_map(
        body, mesh=mesh, in_specs=placed, out_specs=P(("row", "depth"), "col"), check_vma=False
    )
```

time: 35.4 us -> 32.4 us (0.915)
  Pallas kernels: 33.8 us -> 31 us
    pallas_call x1, Pallas kernels: 33.8 us -> 31 us  [local_fast(): call(*(pltpu.with_memory_space_constraint(x, pltpu.HBM) for x in operands))]
where the time goes in v2:
time: 32.4 us; the launch traced here: 32.2 us
  Pallas kernels  31 us (96%)
  local copies, waits for them, and re-layouts  1.15 us (4%)
    pallas_call x1, Pallas kernels, local_fast(): call(*(pltpu.with_memory_space_constraint(x, pltpu.HBM) for x in operands))  31 us
    unnamed x1, local copies, waits for them, and re-layouts  1.15 us

profile of v2, /device:TPU:30, one launch (start us, length us, event | category | flops | bytes accessed | tf_op | source)
XLA Modules:
  0.0 32.2 jit_solution(12557317443889280468)
XLA Ops:
  0.0 31.0 %shard_map.64 = bf16[512,1536]{1,0:T(8,128)(2,1)S(1)} custom-call(s32[2,8]{1,0:T(2,128)} %bitcast.16, s32[1,8]{1,0:T(1,128)} %bitcast.17, s32[4,1,16]{2,1,0:T(1,128)} %bitcast.14, s32[4,1,16]{2,1,0:T(1,128)} %bitcast.15, bf16[8,2,128,128]{3,2,1,0:T(8,128)(2,1)} %bitcast.13, bf16[4,16,128,128]{3,2,1,0:T(8,128)(2,1)} %bitcast.12), custom_call_target="tpu_custom_call" | custom-call | tf_op jit(solution)/shard_map/pallas_call | solution.py:532
  31.0 1.1 %copy.10 = bf16[512,1536]{1,0:T(8,128)(2,1)} copy(bf16[512,1536]{1,0:T(8,128)(2,1)S(1)} %shard_map.64) | data formatting | bytes 3145728

commit v3 on v2

--- a/solution.py
+++ b/solution.py
@@ -244,14 +244,17 @@
 
     own = [a_ref.at[dep * half + r] for r in range(half)] + [unit(0, half + r) for r in range(half)]
 
+    def landed(p, u):
+        return recv_a.at[(p - 1) * units + u]
+
     def to_panel(p, sources, n, dev):
-        return [remote(src, unit(p, u), send_a.at[n], recv_a.at[p, u], dev) for u, src in enumerate(sources)]
+        return [remote(src, unit(p, u), send_a.at[n], landed(p, u), dev) for u, src in enumerate(sources)]
 
     def panel(p):
         return [unit(p, u) for u in range(units)]
 
     swap = [
-        remote(a_ref.at[(1 - dep) * half + r], unit(0, half + r), send_a.at[0], recv_a.at[0, r], twin_dev)
+        remote(a_ref.at[(1 - dep) * half + r], unit(0, half + r), send_a.at[0], landed(REACH, r), twin_dev)
         for r in range(half)
     ]
     chain = to_panel(2, own, 1, down)
@@ -260,9 +263,8 @@
     own_x1 = to_panel(1, own, 4, side_dev)
     fwd_x1 = to_panel(1, panel(2), 4, side_dev)
     fwd_x3 = to_panel(3, panel(2), 5, side_dev)
-    top_x3 = to_panel(3, panel(4), 5, side_dev)
+    top_x3 = to_panel(3, panel(4)[: units - LATE], 5, side_dev)
     low_x3 = to_panel(3, panel(1), 6, down)
-    late = range(units - LATE, units)
 
     near_b = [remote(b_ref.at[m_near[k]], near_twin[k], send_b.at[0], recv_n, twin_dev) for k in range(2)]
     far_b, pass_b = [], []
@@ -270,11 +272,11 @@
         for c in range(CHUNKS):
             part = pl.ds(c * step_b, step_b)
             far_b.append(
-                remote(b_ref.at[m_far[k], part], far_own[k].at[part], send_b.at[1], recv_b.at[k, c], row_dev)
+                remote(b_ref.at[m_far[k], part], far_own[k].at[part], send_b.at[1], recv_b.at[k * CHUNKS + c], row_dev)
             )
             pass_b.append(
                 remote(
-                    far_own[k].at[part], far_twin[k].at[part], send_b.at[2], recv_b.at[2 + k, 0], twin_dev
+                    far_own[k].at[part], far_twin[k].at[part], send_b.at[2], recv_b.at[2 * CHUNKS + k], twin_dev
                 )
             )
 
@@ -292,30 +294,25 @@
     for copy in index_local:
         copy.wait()
     start([swap_m] + swap)
-    first = half // 2
-    start(chain[:first], z > 0)
-    start(own_x1[:first], side1)
+    start(chain[:2], z > 0)
+    start(own_x1[:2], side1)
     pl.when(row0)(lambda: pl.semaphore_wait(ready.at[0], 1))
     start([far_m] + far_b + [near_m] + near_b)
     swap_m.wait_recv()
-    start([chain_m], z > 0)
-    start([own_x1_m], side1)
-    start(chain[first:half], z > 0)
-    start(own_x1[first:half], side1)
-    for r in range(half):
-        swap[r].wait_recv()
-    start(chain[half:], z > 0)
-    start(own_x1[half:], side1)
+    start([chain_m] + chain[2:half], z > 0)
+    start([own_x1_m] + own_x1[2:half], side1)
+    for copy in swap:
+        copy.wait_recv()
 
     @pl.when(z == 0)
     def _():
         pl.semaphore_wait(ready.at[2], 1)
-        start(chain[:first] + [chain_m] + chain[first:])
+        start([chain_m] + chain[:half])
 
     @pl.when(both(row1, z == 1))
     def _():
         pl.semaphore_wait(ready.at[2], 1)
-        start(skip[:1] + [skip_m])
+        start([skip_m] + skip[:1])
 
     pl.when(side0)(lambda: pl.semaphore_wait(ready.at[1], 1))
     run[zero_at] = jnp.zeros(run.shape[1:], jnp.float32)
@@ -326,10 +323,10 @@
 
     def low(u):
         recv(1, u)
-        start([low_x3[u]], side1, *([] if u in late else [row0]))
+        start([low_x3[u]], side1, *([] if u >= units - LATE else [row0]))
 
     def recv(p, u):
-        drain(unit(p, u), recv_a.at[p, u])
+        drain(unit(p, u), landed(p, u))
 
     groups = [(s, m, k, d, far) for k in range(2) for far, s, m in ((0, s_near[k], m_near[k]), (1, s_far[k], m_mine[k]))
               for d in range(2)]
@@ -357,42 +354,45 @@
                 last = jnp.where(c_p == c, r * terms + at_p, last)
             ltab[r * out_cols + c] = last
 
-    def product(g, r, t, right):
+    def products(g, wanted, right):
         s, _, _, d, _ = groups[g]
-        here = r * terms + g * per_row + t
-        left = A[(s + row) * units + d * half + r, t]
-        value = jnp.dot(left, right[ktab[here]], preferred_element_type=jnp.float32)
-        run[here] = value + run[ptab[here]]
+        values = []
+        for r, t in wanted:
+            here = r * terms + g * per_row + t
+            left = A[(s + row) * units + d * half + r, t]
+            values.append((here, jnp.dot(left, right[ktab[here]], preferred_element_type=jnp.float32)))
+        for here, value in values:
+            run[here] = value + run[ptab[here]]
+
+    def unit_of(g, r, right):
+        products(g, [(r, t) for t in range(per_row)], right)
 
     def whole_group(g, right):
-        def one(t, carry):
-            for r in range(half):
-                product(g, r, t, right)
-            return carry
-
-        lax.fori_loop(0, per_row, one, 0)
-
-    def unit_of(g, r, right):
-        for t in range(per_row):
-            product(g, r, t, right)
+        for r in range(half):
+            unit_of(g, r, right)
 
     for u in range(units):
         recv(2, u)
-        start([chain2[u]], row1, z > 0)
-        start([fwd_x1[u]], side0)
-        start([fwd_x3[u]], side1)
         if u == 0:
             drain(MA.at[pl.ds(4, 2)], recv_m.at[2])
             start([chain2_m], row1, z > 0)
             start([fwd_x1_m], side0)
             start([fwd_x3_m], side1)
+        start([fwd_x1[u]], side0)
+        if u == 2:
+            drain(MA.at[pl.ds(2, 2)], recv_m.at[1])
+            start([low_x3_m], side1)
+        if u < half:
+            start([chain[half + u]])
+            start([own_x1[half + u]], side1)
+        else:
+            start(chain2[2 * (u - half) : 2 * (u - half) + 2], row1, z > 0)
+            start(fwd_x3[2 * (u - half) : 2 * (u - half) + 2], side1)
+        if u == 0:
             far_m.wait_recv()
             pass_m.start()
-        if u == units - 2:
+        if u == units - 3:
             start(skip[1:], row1, z == 1)
-        if u == units // 2:
-            drain(MA.at[pl.ds(2, 2)], recv_m.at[1])
-            start([low_x3_m], side1)
         if u >= 3:
             low(u - 3)
         if u % 2:
@@ -403,12 +403,13 @@
         pl.when(both(row1, side1))(lambda: recv(4, u))
         unit_of(4 + u // half, u % half, (Bn1, Gn1)[u // half])
 
-    near_done = 0
+    scalars = [pltpu.make_async_copy(MA, SA, local_sem.at[0]), pltpu.make_async_copy(MB, SB, local_sem.at[1])]
+
     for u in range(units):
         @pl.when(both(row1, side0))
         def _():
             recv(4, u)
-            if u not in late:
+            if u < units - LATE:
                 top_x3[u].start()
 
         if u < 3:
@@ -418,49 +419,59 @@
             pl.when(row1)(lambda: drain(MA.at[pl.ds(8, 2)], recv_m.at[4]))
             near_m.wait_recv()
             pass_m.wait_recv()
-            scalars = [pltpu.make_async_copy(MA, SA, local_sem.at[0]), pltpu.make_async_copy(MB, SB, local_sem.at[1])]
             start(scalars)
-            for copy in scalars:
-                copy.wait()
-            for copy in b_local + [a_local]:
+        if u == 1:
+            for copy in scalars + b_local + [a_local]:
                 copy.wait()
             drain(A.at[pl.ds(0, 2 * units)], recv_n)
-            drain(A.at[pl.ds(0, units)], recv_b.at[2, 0])
-        if u % 2:
+            drain(A.at[pl.ds(0, units)], recv_b.at[2 * CHUNKS])
+        if u in (1, 3, 5):
             far_part(CHUNKS + u // 2)
-        if 1 <= u <= half:
-            tables(u - 1)
-        if u == half:
+        if u in (1, 2):
+            for r in range((u - 1) * half // 2, u * half // 2):
+                tables(r)
+        if u == 3:
             whole_group(0, Bn0)
-        if u == half + 1:
+        if u == 4:
             whole_group(1, Gn0)
             whole_group(2, Bf0)
-        if u == half + 2:
+        if u == 5:
             whole_group(3, Gf0)
-        if u > half + 1:
-            for w in range(near_done, near_done + 3):
+        if u == 6:
+            for w in range(half):
                 near_unit(w)
-            near_done += 3
-    for u in range(near_done, units):
-        near_unit(u)
-
-    def far_unit(u, right):
+        if u == 7:
+            for w in range(half, units - 2):
+                near_unit(w)
+    far_part(2 * CHUNKS - 1)
+
+    def far_unit(u):
         pl.when(row == side)(lambda: recv(3, u))
-        unit_of(6 + u // half, u % half, right)
-
-    for u in range(half):
-        far_unit(u, Bf1)
-    drain(A.at[pl.ds(0, units)], recv_b.at[3, 0])
-    for u in range(half, units):
-        far_unit(u, Gf1)
-
-    def place(r, carry):
-        rows = pl.ds(pl.multiple_of(r * size, size), size)
+        unit_of(6 + u // half, u % half, (Bf1, Gf1)[u // half])
+
+    def place(r):
         for c in range(out_cols):
-            out_ref[rows, c * size : (c + 1) * size] = run[ltab[r * out_cols + c]].astype(out_ref.dtype)
-        return carry
-
-    lax.fori_loop(0, half, place, 0)
+            out_ref[r * size : (r + 1) * size, c * size : (c + 1) * size] = run[ltab[r * out_cols + c]].astype(
+                out_ref.dtype
+            )
+
+    def last_row():
+        near_unit(units - 1)
+        far_unit(half - 1)
+
+    for r in range(half - 2):
+        far_unit(r)
+    near_unit(units - 2)
+    far_unit(half - 2)
+    pl.when(z < top)(last_row)
+    drain(A.at[pl.ds(0, units)], recv_b.at[2 * CHUNKS + 1])
+    for r in range(half - 2):
+        far_unit(half + r)
+        place(r)
+    pl.when(z == top)(last_row)
+    for r in range(half - 2, half):
+        far_unit(half + r)
+        place(r)
 
     def sent(n, sem, *flags):
         if flags:
@@ -510,9 +521,9 @@
             pltpu.SemaphoreType.DMA((5,)),
             pltpu.SemaphoreType.DMA((8,)),
             pltpu.SemaphoreType.DMA((7,)),
-            pltpu.SemaphoreType.DMA((REACH, block_rows)),
+            pltpu.SemaphoreType.DMA((SHIFTS * block_rows + half,)),
             pltpu.SemaphoreType.DMA((3,)),
-            pltpu.SemaphoreType.DMA((4, CHUNKS)),
+            pltpu.SemaphoreType.DMA((2 * CHUNKS + 2,)),
             pltpu.SemaphoreType.DMA,
             pltpu.SemaphoreType.REGULAR((3,)),
             pltpu.SemaphoreType.DMA((7,)),

time: 32.4 us -> 32.1 us (level)
  Pallas kernels: 31 us -> 30.5 us
    pallas_call x1, Pallas kernels: 31 us -> 30.5 us  [local_fast(): call(*(pltpu.with_memory_space_constraint(x, pltpu.HBM) for x in operands))]
where the time goes in v3:
time: 32.1 us; the launch traced here: 31.6 us
  Pallas kernels  30.5 us (95%)
  local copies, waits for them, and re-layouts  1.15 us (4%)
    pallas_call x1, Pallas kernels, local_fast(): call(*(pltpu.with_memory_space_constraint(x, pltpu.HBM) for x in operands))  30.5 us
    unnamed x1, local copies, waits for them, and re-layouts  1.15 us

profile of v3, /device:TPU:30, one launch (start us, length us, event | category | flops | bytes accessed | tf_op | source)
XLA Modules:
  0.0 31.6 jit_solution(8644609087785298884)
XLA Ops:
  0.0 30.5 %shard_map.64 = bf16[512,1536]{1,0:T(8,128)(2,1)S(1)} custom-call(s32[2,8]{1,0:T(2,128)} %bitcast.16, s32[1,8]{1,0:T(1,128)} %bitcast.17, s32[4,1,16]{2,1,0:T(1,128)} %bitcast.14, s32[4,1,16]{2,1,0:T(1,128)} %bitcast.15, bf16[8,2,128,128]{3,2,1,0:T(8,128)(2,1)} %bitcast.13, bf16[4,16,128,128]{3,2,1,0:T(8,128)(2,1)} %bitcast.12), custom_call_target="tpu_custom_call" | custom-call | tf_op jit(solution)/shard_map/pallas_call | solution.py:543
  30.5 1.1 %copy.10 = bf16[512,1536]{1,0:T(8,128)(2,1)} copy(bf16[512,1536]{1,0:T(8,128)(2,1)S(1)} %shard_map.64) | data formatting | bytes 3145728

commit v4 on v3

--- a/solution.py
+++ b/solution.py
@@ -142,14 +142,14 @@
 
 
 REACH = SHIFTS + 1
-CHUNKS = 4
+PARTS = ((8, 8), (7, 6, 3))
 LATE = 1
 MESH_ID = pl.DeviceIdType.MESH
 
 
 def gather_multiply(n_col, a_cols, a_count, b_cols, b_count, a_ref, b_ref, out_ref, A, Bn0, Bn1, Bf0, Bf1,
                     Gn0, Gn1, Gf0, Gf1, MA, MB, SA, SB, run, ktab, ptab, ltab,
-                    send_m, recv_m, send_a, recv_a, send_b, recv_b, recv_n, ready, local_sem):
+                    send_m, recv_m, send_a, recv_a, send_b, recv_b, passed, ready, local_sem):
     row = lax.axis_index("row")
     col = lax.axis_index("col")
     dep = lax.axis_index("depth")
@@ -163,7 +163,6 @@
     out_cols = out_ref.shape[1] // size
     terms = SHIFTS * 2 * per_row
     zero_at = half * terms
-    step_b = inner // CHUNKS
     row0, row1, side0, side1 = row == 0, row == 1, side == 0, side == 1
 
     def both(*flags):
@@ -211,13 +210,13 @@
 
     index_local = [
         pltpu.make_async_copy(src, dst, local_sem.at[n])
-        for n, (src, dst) in enumerate((
-            (a_cols, MA.at[0, pl.ds(0, per_row)]), (a_count, MA.at[0, pl.ds(per_row, 1)]),
-            (b_cols, MB.at[0, 0]), (b_count, MB.at[0, 1]),
-        ))
+        for src, dst, n in (
+            (a_cols, MA.at[0, pl.ds(0, per_row)], 0), (a_count, MA.at[0, pl.ds(per_row, 1)], 0),
+            (b_cols, MB.at[0, 0], 1), (b_count, MB.at[0, 1], 1),
+        )
     ]
-    b_local = [pltpu.make_async_copy(b_ref.at[m_near[k]], near_own[k], local_sem.at[4 + k]) for k in range(2)]
-    a_local = pltpu.make_async_copy(a_ref.at[pl.ds(dep * half, half)], A.at[pl.ds(0, half)], local_sem.at[6])
+    b_local = [pltpu.make_async_copy(b_ref.at[m_near[k]], near_own[k], local_sem.at[2]) for k in range(2)]
+    a_local = pltpu.make_async_copy(a_ref.at[pl.ds(dep * half, half)], A.at[pl.ds(0, half)], local_sem.at[2])
     start(index_local + b_local + [a_local])
 
     @pl.when(row0)
@@ -245,7 +244,7 @@
     own = [a_ref.at[dep * half + r] for r in range(half)] + [unit(0, half + r) for r in range(half)]
 
     def landed(p, u):
-        return recv_a.at[(p - 1) * units + u]
+        return recv_a.at[(SHIFTS - 1) * units + u // 2 if p == 1 else (p - 2) * units + u]
 
     def to_panel(p, sources, n, dev):
         return [remote(src, unit(p, u), send_a.at[n], landed(p, u), dev) for u, src in enumerate(sources)]
@@ -254,45 +253,41 @@
         return [unit(p, u) for u in range(units)]
 
     swap = [
-        remote(a_ref.at[(1 - dep) * half + r], unit(0, half + r), send_a.at[0], landed(REACH, r), twin_dev)
+        remote(a_ref.at[(1 - dep) * half + r], unit(0, half + r), send_a.at[0], recv_a.at[(SHIFTS - 1) * units + half + r // 2], twin_dev)
         for r in range(half)
     ]
-    chain = to_panel(2, own, 1, down)
-    chain2 = to_panel(4, panel(2), 2, down)
-    skip = to_panel(4, own, 3, down2)
-    own_x1 = to_panel(1, own, 4, side_dev)
-    fwd_x1 = to_panel(1, panel(2), 4, side_dev)
-    fwd_x3 = to_panel(3, panel(2), 5, side_dev)
-    top_x3 = to_panel(3, panel(4)[: units - LATE], 5, side_dev)
-    low_x3 = to_panel(3, panel(1), 6, down)
-
-    near_b = [remote(b_ref.at[m_near[k]], near_twin[k], send_b.at[0], recv_n, twin_dev) for k in range(2)]
+    chain = to_panel(2, own, 0, down)
+    chain2 = to_panel(4, panel(2), 1, down)
+    skip = to_panel(4, own, 1, down2)
+    own_x1 = to_panel(1, own, 0, side_dev)
+    fwd_x1 = to_panel(1, panel(2), 0, side_dev)
+    fwd_x3 = to_panel(3, panel(2), 2, side_dev)
+    top_x3 = to_panel(3, panel(4)[: units - LATE], 2, side_dev)
+    low_x3 = to_panel(3, panel(1), 2, down)
+
+    near_b = [remote(b_ref.at[m_near[k]], near_twin[k], send_b, passed.at[2], twin_dev) for k in range(2)]
     far_b, pass_b = [], []
-    for k in range(2):
-        for c in range(CHUNKS):
-            part = pl.ds(c * step_b, step_b)
+    for k, sizes in enumerate(PARTS):
+        for c, blocks in enumerate(sizes):
+            part = pl.ds(sum(sizes[:c]) * inner // 16, blocks * inner // 16)
             far_b.append(
-                remote(b_ref.at[m_far[k], part], far_own[k].at[part], send_b.at[1], recv_b.at[k * CHUNKS + c], row_dev)
+                remote(b_ref.at[m_far[k], part], far_own[k].at[part], send_b, recv_b.at[len(far_b)], row_dev)
             )
-            pass_b.append(
-                remote(
-                    far_own[k].at[part], far_twin[k].at[part], send_b.at[2], recv_b.at[2 * CHUNKS + k], twin_dev
-                )
-            )
+            pass_b.append(remote(far_own[k].at[part], far_twin[k].at[part], send_b, passed.at[k], twin_dev))
 
     def index_a(src, dst, n, sem, dev):
-        return remote(MA.at[pl.ds(src, n)], MA.at[pl.ds(dst, n)], send_m.at[sem], recv_m.at[dst // 2], dev)
+        return remote(MA.at[pl.ds(src, n)], MA.at[pl.ds(dst, n)], send_m.at[sem], recv_m.at[min(dst // 2, 3)], dev)
 
     swap_m = remote(MA.at[0], MA.at[1], send_m.at[0], recv_m.at[0], twin_dev)
-    near_m = remote(MB.at[0], MB.at[1], send_m.at[1], recv_m.at[5], twin_dev)
-    far_m = remote(MB.at[0], MB.at[2], send_m.at[1], recv_m.at[6], row_dev)
-    pass_m = remote(MB.at[2], MB.at[3], send_m.at[1], recv_m.at[7], twin_dev)
+    near_m = remote(MB.at[0], MB.at[1], send_m.at[1], recv_m.at[4], twin_dev)
+    far_m = remote(MB.at[0], MB.at[2], send_m.at[1], recv_m.at[5], row_dev)
+    pass_m = remote(MB.at[2], MB.at[3], send_m.at[1], recv_m.at[4], twin_dev)
     chain_m, chain2_m, skip_m = index_a(0, 4, 2, 0, down), index_a(4, 8, 2, 2, down), index_a(0, 8, 2, 3, down2)
     own_x1_m, fwd_x1_m = index_a(0, 2, 2, 0, side_dev), index_a(4, 2, 2, 0, side_dev)
     fwd_x3_m, low_x3_m = index_a(4, 6, 2, 4, side_dev), index_a(2, 6, 2, 4, down)
 
-    for copy in index_local:
-        copy.wait()
+    drain(MA.at[0], local_sem.at[0])
+    drain(MB.at[0], local_sem.at[1])
     start([swap_m] + swap)
     start(chain[:2], z > 0)
     start(own_x1[:2], side1)
@@ -301,8 +296,8 @@
     swap_m.wait_recv()
     start([chain_m] + chain[2:half], z > 0)
     start([own_x1_m] + own_x1[2:half], side1)
-    for copy in swap:
-        copy.wait_recv()
+    for n in range(half // 2):
+        drain(A.at[pl.ds(0, 2)], recv_a.at[(SHIFTS - 1) * units + half + n])
 
     @pl.when(z == 0)
     def _():
@@ -312,7 +307,7 @@
     @pl.when(both(row1, z == 1))
     def _():
         pl.semaphore_wait(ready.at[2], 1)
-        start([skip_m] + skip[:1])
+        start([skip_m] + skip)
 
     pl.when(side0)(lambda: pl.semaphore_wait(ready.at[1], 1))
     run[zero_at] = jnp.zeros(run.shape[1:], jnp.float32)
@@ -322,8 +317,9 @@
         pass_b[n].start()
 
     def low(u):
-        recv(1, u)
-        start([low_x3[u]], side1, *([] if u >= units - LATE else [row0]))
+        drain(A.at[pl.ds(0, 2)], landed(1, u))
+        for w in (u, u + 1):
+            start([low_x3[w]], side1, *([] if w >= units - LATE else [row0]))
 
     def recv(p, u):
         drain(unit(p, u), landed(p, u))
@@ -354,22 +350,23 @@
                 last = jnp.where(c_p == c, r * terms + at_p, last)
             ltab[r * out_cols + c] = last
 
-    def products(g, wanted, right):
-        s, _, _, d, _ = groups[g]
-        values = []
-        for r, t in wanted:
-            here = r * terms + g * per_row + t
-            left = A[(s + row) * units + d * half + r, t]
-            values.append((here, jnp.dot(left, right[ktab[here]], preferred_element_type=jnp.float32)))
-        for here, value in values:
-            run[here] = value + run[ptab[here]]
-
-    def unit_of(g, r, right):
-        products(g, [(r, t) for t in range(per_row)], right)
-
-    def whole_group(g, right):
-        for r in range(half):
-            unit_of(g, r, right)
+    rights = (Bn0, Gn0, Bf0, Gf0, Bn1, Gn1, Bf1, Gf1)
+
+    def products(wanted):
+        held = None
+        for g, r in wanted:
+            s, _, _, d, _ = groups[g]
+            for t in range(per_row):
+                here = r * terms + g * per_row + t
+                left = A[(s + row) * units + d * half + r, t]
+                value = jnp.dot(left, rights[g][ktab[here]], preferred_element_type=jnp.float32)
+                if held is not None:
+                    run[held[0]] = held[1] + run[ptab[held[0]]]
+                held = here, value
+        run[held[0]] = held[1] + run[ptab[held[0]]]
+
+    def whole_group(g):
+        products([(g, r) for r in range(half)])
 
     for u in range(units):
         recv(2, u)
@@ -391,87 +388,109 @@
         if u == 0:
             far_m.wait_recv()
             pass_m.start()
-        if u == units - 3:
-            start(skip[1:], row1, z == 1)
-        if u >= 3:
-            low(u - 3)
-        if u % 2:
-            far_part(u // 2)
-
-    def near_unit(u):
-        pl.when(row != side)(lambda: recv(3, u))
-        pl.when(both(row1, side1))(lambda: recv(4, u))
-        unit_of(4 + u // half, u % half, (Bn1, Gn1)[u // half])
+        if u in (4, 6):
+            low(u - 4)
+        if u in (3, 7):
+            far_part(u // 4)
+
+    def near_units(*wanted):
+        @pl.when(row != side)
+        def _():
+            for u in wanted:
+                recv(3, u)
+
+        @pl.when(both(row1, side1))
+        def _():
+            for u in wanted:
+                recv(4, u)
+
+        products([(4 + u // half, u % half) for u in wanted])
+
+    def far_units(*wanted):
+        @pl.when(row == side)
+        def _():
+            for u in wanted:
+                recv(3, u)
+
+        if units - 1 in wanted:
+            pl.when(both(row1, side0))(lambda: recv(4, units - 1))
+        products([(6 + u // half, u % half) for u in wanted])
 
     scalars = [pltpu.make_async_copy(MA, SA, local_sem.at[0]), pltpu.make_async_copy(MB, SB, local_sem.at[1])]
 
     for u in range(units):
-        @pl.when(both(row1, side0))
-        def _():
-            recv(4, u)
-            if u < units - LATE:
+        if u < units - LATE:
+            @pl.when(both(row1, side0))
+            def _():
+                recv(4, u)
                 top_x3[u].start()
 
-        if u < 3:
-            low(units - 3 + u)
+        if u in (0, 2):
+            low(half + u)
         if u == 0:
-            drain(MA.at[pl.ds(6, 2)], recv_m.at[3])
-            pl.when(row1)(lambda: drain(MA.at[pl.ds(8, 2)], recv_m.at[4]))
-            near_m.wait_recv()
-            pass_m.wait_recv()
+            pl.when(row0)(lambda: drain(MA.at[pl.ds(6, 2)], recv_m.at[3]))
+            pl.when(row1)(lambda: drain(MA.at[pl.ds(6, 4)], recv_m.at[3]))
+            drain(MB.at[pl.ds(0, 2)], recv_m.at[4])
             start(scalars)
         if u == 1:
-            for copy in scalars + b_local + [a_local]:
+            for copy in scalars:
                 copy.wait()
-            drain(A.at[pl.ds(0, 2 * units)], recv_n)
-            drain(A.at[pl.ds(0, units)], recv_b.at[2 * CHUNKS])
-        if u in (1, 3, 5):
-            far_part(CHUNKS + u // 2)
+            drain(A.at[pl.ds(0, 2 * units + half)], local_sem.at[2])
+            drain(A.at[pl.ds(0, 2 * units)], passed.at[2])
+            drain(A.at[pl.ds(0, units)], passed.at[0])
+        if u in (3, 5):
+            far_part((u + 1) // 2)
         if u in (1, 2):
             for r in range((u - 1) * half // 2, u * half // 2):
                 tables(r)
+        if u == 2:
+            whole_group(0)
         if u == 3:
-            whole_group(0, Bn0)
+            whole_group(1)
+            whole_group(2)
         if u == 4:
-            whole_group(1, Gn0)
-            whole_group(2, Bf0)
+            whole_group(3)
+            near_units(0)
         if u == 5:
-            whole_group(3, Gf0)
+            near_units(1, 2)
         if u == 6:
-            for w in range(half):
-                near_unit(w)
-        if u == 7:
-            for w in range(half, units - 2):
-                near_unit(w)
-    far_part(2 * CHUNKS - 1)
-
-    def far_unit(u):
-        pl.when(row == side)(lambda: recv(3, u))
-        unit_of(6 + u // half, u % half, (Bf1, Gf1)[u // half])
-
-    def place(r):
-        for c in range(out_cols):
-            out_ref[r * size : (r + 1) * size, c * size : (c + 1) * size] = run[ltab[r * out_cols + c]].astype(
-                out_ref.dtype
-            )
-
-    def last_row():
-        near_unit(units - 1)
-        far_unit(half - 1)
-
-    for r in range(half - 2):
-        far_unit(r)
-    near_unit(units - 2)
-    far_unit(half - 2)
-    pl.when(z < top)(last_row)
-    drain(A.at[pl.ds(0, units)], recv_b.at[2 * CHUNKS + 1])
-    for r in range(half - 2):
-        far_unit(half + r)
-        place(r)
-    pl.when(z == top)(last_row)
-    for r in range(half - 2, half):
-        far_unit(half + r)
-        place(r)
+            near_units(3, 4)
+    far_part(len(far_b) - 1)
+
+    def place(*rows):
+        for r in rows:
+            for c in range(out_cols):
+                out_ref[r * size : (r + 1) * size, c * size : (c + 1) * size] = run[ltab[r * out_cols + c]].astype(
+                    out_ref.dtype
+                )
+
+    def last_pass():
+        drain(A.at[pl.ds(0, units)], passed.at[1])
+
+    @pl.when(z < top)
+    def _():
+        near_units(5, 6, 7)
+        far_units(0, 1, 2, 3)
+        last_pass()
+        far_units(4, 5, 6, 7)
+        place(0, 1, 2, 3)
+
+    @pl.when(z == top)
+    def _():
+        far_units(0)
+        near_units(5)
+        far_units(1)
+        last_pass()
+        far_units(4, 5)
+        place(0, 1)
+        near_units(6)
+        far_units(2)
+        far_units(6)
+        place(2)
+        near_units(7)
+        far_units(3)
+        far_units(7)
+        place(3)
 
     def sent(n, sem, *flags):
         if flags:
@@ -479,17 +498,13 @@
         else:
             drain(A.at[pl.ds(0, n)], sem)
 
-    sent(half, send_a.at[0])
-    sent(units, send_a.at[1])
-    sent(units, send_a.at[2], row1, z > 0)
-    sent(units, send_a.at[3], row1, z == 1)
-    sent(units, send_a.at[4])
-    sent(units, send_a.at[5], side1)
-    sent(units - LATE, send_a.at[5], side0, row1)
-    sent(units, send_a.at[6], side1, row0)
-    sent(LATE, send_a.at[6], side1, row1)
-    for n in range(3):
-        sent(2 * units, send_b.at[n])
+    sent(2 * units + half, send_a.at[0])
+    sent(units, send_a.at[1], row1, z > 1)
+    sent(2 * units, send_a.at[1], row1, z == 1)
+    sent(2 * units, send_a.at[2], side1, row0)
+    sent(units + LATE, send_a.at[2], side1, row1)
+    sent(units - LATE, send_a.at[2], side0, row1)
+    drain(run.at[pl.ds(0, 6 * units)], send_b)
     drain(MA.at[pl.ds(0, 5)], send_m.at[0])
     drain(MB.at[pl.ds(0, 3)], send_m.at[1])
     pl.when(both(row1, z > 0))(lambda: drain(MA.at[pl.ds(0, 2)], send_m.at[2]))
@@ -519,14 +534,14 @@
             pltpu.SMEM((count,), jnp.int32),
             pltpu.SMEM((half * BC,), jnp.int32),
             pltpu.SemaphoreType.DMA((5,)),
-            pltpu.SemaphoreType.DMA((8,)),
-            pltpu.SemaphoreType.DMA((7,)),
-            pltpu.SemaphoreType.DMA((SHIFTS * block_rows + half,)),
+            pltpu.SemaphoreType.DMA((6,)),
             pltpu.SemaphoreType.DMA((3,)),
-            pltpu.SemaphoreType.DMA((2 * CHUNKS + 2,)),
+            pltpu.SemaphoreType.DMA(((SHIFTS - 1) * block_rows + half + half // 2,)),
             pltpu.SemaphoreType.DMA,
+            pltpu.SemaphoreType.DMA((sum(map(len, PARTS)),)),
+            pltpu.SemaphoreType.DMA((3,)),
             pltpu.SemaphoreType.REGULAR((3,)),
-            pltpu.SemaphoreType.DMA((7,)),
+            pltpu.SemaphoreType.DMA((3,)),
         ],
         compiler_params=pltpu.CompilerParams(
             collective_id=0, has_side_effects=True, vmem_limit_bytes=40 * 1024 * 1024

time: 32.1 us -> 31.9 us (level)
  no operation moved by 1% of the time
where the time goes in v4:
time: 31.9 us; the launch traced here: 31.7 us
  Pallas kernels  30.6 us (96%)
  local copies, waits for them, and re-layouts  1.15 us (4%)
    pallas_call x1, Pallas kernels, local_fast(): call(*(pltpu.with_memory_space_constraint(x, pltpu.HBM) for x in operands))  30.6 us
    unnamed x1, local copies, waits for them, and re-layouts  1.15 us

profile of v4, /device:TPU:30, one launch (start us, length us, event | category | flops | bytes accessed | tf_op | source)
XLA Modules:
  0.0 31.7 jit_solution(16344290989517388060)
XLA Ops:
  0.0 30.6 %shard_map.64 = bf16[512,1536]{1,0:T(8,128)(2,1)S(1)} custom-call(s32[2,8]{1,0:T(2,128)} %bitcast.16, s32[1,8]{1,0:T(1,128)} %bitcast.17, s32[4,1,16]{2,1,0:T(1,128)} %bitcast.14, s32[4,1,16]{2,1,0:T(1,128)} %bitcast.15, bf16[8,2,128,128]{3,2,1,0:T(8,128)(2,1)} %bitcast.13, bf16[4,16,128,128]{3,2,1,0:T(8,128)(2,1)} %bitcast.12), custom_call_target="tpu_custom_call" | custom-call | tf_op jit(solution)/shard_map/pallas_call | solution.py:558
  30.6 1.1 %copy.10 = bf16[512,1536]{1,0:T(8,128)(2,1)} copy(bf16[512,1536]{1,0:T(8,128)(2,1)S(1)} %shard_map.64) | data formatting | bytes 3145728

commit v5 on v4

--- a/solution.py
+++ b/solution.py
@@ -144,12 +144,13 @@
 REACH = SHIFTS + 1
 PARTS = ((8, 8), (7, 6, 3))
 LATE = 1
+SPLIT = 6
 MESH_ID = pl.DeviceIdType.MESH
 
 
 def gather_multiply(n_col, a_cols, a_count, b_cols, b_count, a_ref, b_ref, out_ref, A, Bn0, Bn1, Bf0, Bf1,
                     Gn0, Gn1, Gf0, Gf1, MA, MB, SA, SB, run, ktab, ptab, ltab,
-                    send_m, recv_m, send_a, recv_a, send_b, recv_b, passed, ready, local_sem):
+                    send_m, recv_m, send_a, recv_a, send_b, recv_b, passed, halves, ready, local_sem):
     row = lax.axis_index("row")
     col = lax.axis_index("col")
     dep = lax.axis_index("depth")
@@ -246,8 +247,17 @@
     def landed(p, u):
         return recv_a.at[(SHIFTS - 1) * units + u // 2 if p == 1 else (p - 2) * units + u]
 
-    def to_panel(p, sources, n, dev):
-        return [remote(src, unit(p, u), send_a.at[n], landed(p, u), dev) for u, src in enumerate(sources)]
+    def to_panel(p, sources, n, dev, split=-1):
+        copies = []
+        for u, src in enumerate(sources):
+            dst = unit(p, u)
+            if u == split:
+                for t in range(per_row):
+                    sem = halves.at[t] if p == SHIFTS else landed(p, u)
+                    copies.append(remote(src.at[t], dst.at[t], send_a.at[n], sem, dev))
+            else:
+                copies.append(remote(src, dst, send_a.at[n], landed(p, u), dev))
+        return copies
 
     def panel(p):
         return [unit(p, u) for u in range(units)]
@@ -257,12 +267,12 @@
         for r in range(half)
     ]
     chain = to_panel(2, own, 0, down)
-    chain2 = to_panel(4, panel(2), 1, down)
-    skip = to_panel(4, own, 1, down2)
+    chain2 = to_panel(4, panel(2), 1, down, SPLIT)
+    skip = to_panel(4, own, 1, down2, SPLIT)
     own_x1 = to_panel(1, own, 0, side_dev)
     fwd_x1 = to_panel(1, panel(2), 0, side_dev)
     fwd_x3 = to_panel(3, panel(2), 2, side_dev)
-    top_x3 = to_panel(3, panel(4)[: units - LATE], 2, side_dev)
+    top_x3 = to_panel(3, panel(4)[: units - LATE], 2, side_dev, SPLIT)
     low_x3 = to_panel(3, panel(1), 2, down)
 
     near_b = [remote(b_ref.at[m_near[k]], near_twin[k], send_b, passed.at[2], twin_dev) for k in range(2)]
@@ -322,7 +332,11 @@
             start([low_x3[w]], side1, *([] if w >= units - LATE else [row0]))
 
     def recv(p, u):
-        drain(unit(p, u), landed(p, u))
+        if p == 4 and u == SPLIT:
+            for t in range(per_row):
+                drain(unit(p, u).at[t], halves.at[t])
+        else:
+            drain(unit(p, u), landed(p, u))
 
     groups = [(s, m, k, d, far) for k in range(2) for far, s, m in ((0, s_near[k], m_near[k]), (1, s_far[k], m_mine[k]))
               for d in range(2)]
@@ -383,7 +397,7 @@
             start([chain[half + u]])
             start([own_x1[half + u]], side1)
         else:
-            start(chain2[2 * (u - half) : 2 * (u - half) + 2], row1, z > 0)
+            start(chain2[2 * (u - half) : 2 * (u - half) + 2 + (u == units - 1)], row1, z > 0)
             start(fwd_x3[2 * (u - half) : 2 * (u - half) + 2], side1)
         if u == 0:
             far_m.wait_recv()
@@ -422,8 +436,13 @@
         if u < units - LATE:
             @pl.when(both(row1, side0))
             def _():
-                recv(4, u)
-                top_x3[u].start()
+                if u == SPLIT:
+                    for t in range(per_row):
+                        drain(unit(4, u).at[t], halves.at[t])
+                        top_x3[u + t].start()
+                else:
+                    recv(4, u)
+                    top_x3[u].start()
 
         if u in (0, 2):
             low(half + u)
@@ -453,8 +472,6 @@
             near_units(0)
         if u == 5:
             near_units(1, 2)
-        if u == 6:
-            near_units(3, 4)
     far_part(len(far_b) - 1)
 
     def place(*rows):
@@ -467,30 +484,39 @@
     def last_pass():
         drain(A.at[pl.ds(0, units)], passed.at[1])
 
-    @pl.when(z < top)
+    @pl.when(side0)
     def _():
-        near_units(5, 6, 7)
+        near_units(3, 4, 5, 6, 7)
         far_units(0, 1, 2, 3)
         last_pass()
         far_units(4, 5, 6, 7)
         place(0, 1, 2, 3)
 
-    @pl.when(z == top)
+    @pl.when(both(side1, z < top))
     def _():
+        near_units(3, 4, 5, 6, 7)
+        far_units(0, 1, 2, 3)
+        last_pass()
+        far_units(4, 5)
+        place(0, 1)
+        far_units(6, 7)
+        place(2, 3)
+
+    @pl.when(both(side1, z == top))
+    def _():
+        near_units(3, 4)
         far_units(0)
         near_units(5)
         far_units(1)
         last_pass()
+        near_units(6)
+        far_units(2)
         far_units(4, 5)
         place(0, 1)
-        near_units(6)
-        far_units(2)
-        far_units(6)
-        place(2)
         near_units(7)
         far_units(3)
-        far_units(7)
-        place(3)
+        far_units(6, 7)
+        place(2, 3)
 
     def sent(n, sem, *flags):
         if flags:
@@ -540,6 +566,7 @@
             pltpu.SemaphoreType.DMA,
             pltpu.SemaphoreType.DMA((sum(map(len, PARTS)),)),
             pltpu.SemaphoreType.DMA((3,)),
+            pltpu.SemaphoreType.DMA((per_row,)),
             pltpu.SemaphoreType.REGULAR((3,)),
             pltpu.SemaphoreType.DMA((3,)),
         ],

time: 31.9 us -> 31.4 us (0.984)
  Pallas kernels: 30.6 us -> 30.1 us
    pallas_call x1, Pallas kernels: 30.6 us -> 30.1 us  [local_fast(): call(*(pltpu.with_memory_space_constraint(x, pltpu.HBM) for x in operands))]
where the time goes in v5:
time: 31.4 us; the launch traced here: 31.3 us
  Pallas kernels  30.1 us (96%)
  local copies, waits for them, and re-layouts  1.15 us (4%)
    pallas_call x1, Pallas kernels, local_fast(): call(*(pltpu.with_memory_space_constraint(x, pltpu.HBM) for x in operands))  30.1 us
    unnamed x1, local copies, waits for them, and re-layouts  1.15 us

profile of v5, /device:TPU:30, one launch (start us, length us, event | category | flops | bytes accessed | tf_op | source)
XLA Modules:
  0.0 31.3 jit_solution(2821635869292982740)
XLA Ops:
  0.0 30.1 %shard_map.64 = bf16[512,1536]{1,0:T(8,128)(2,1)S(1)} custom-call(s32[2,8]{1,0:T(2,128)} %bitcast.16, s32[1,8]{1,0:T(1,128)} %bitcast.17, s32[4,1,16]{2,1,0:T(1,128)} %bitcast.14, s32[4,1,16]{2,1,0:T(1,128)} %bitcast.15, bf16[8,2,128,128]{3,2,1,0:T(8,128)(2,1)} %bitcast.13, bf16[4,16,128,128]{3,2,1,0:T(8,128)(2,1)} %bitcast.12), custom_call_target="tpu_custom_call" | custom-call | tf_op jit(solution)/shard_map/pallas_call | solution.py:585
  30.1 1.1 %copy.10 = bf16[512,1536]{1,0:T(8,128)(2,1)} copy(bf16[512,1536]{1,0:T(8,128)(2,1)S(1)} %shard_map.64) | data formatting | bytes 3145728

commit v6 on v5

--- a/solution.py
+++ b/solution.py
@@ -142,15 +142,17 @@
 
 
 REACH = SHIFTS + 1
-PARTS = ((8, 8), (7, 6, 3))
+PARTS = ((16,), (7, 6, 3))
 LATE = 1
 SPLIT = 6
+FIRST = 3
 MESH_ID = pl.DeviceIdType.MESH
 
 
 def gather_multiply(n_col, a_cols, a_count, b_cols, b_count, a_ref, b_ref, out_ref, A, Bn0, Bn1, Bf0, Bf1,
                     Gn0, Gn1, Gf0, Gf1, MA, MB, SA, SB, run, ktab, ptab, ltab,
-                    send_m, recv_m, send_a, recv_a, send_b, recv_b, passed, halves, ready, local_sem):
+                    send_m, recv_m, send_a, recv_1, recv_2, recv_3, recv_4, swapped, send_b, recv_b, passed, ready,
+                    local_sem):
     row = lax.axis_index("row")
     col = lax.axis_index("col")
     dep = lax.axis_index("depth")
@@ -245,37 +247,37 @@
     own = [a_ref.at[dep * half + r] for r in range(half)] + [unit(0, half + r) for r in range(half)]
 
     def landed(p, u):
-        return recv_a.at[(SHIFTS - 1) * units + u // 2 if p == 1 else (p - 2) * units + u]
-
-    def to_panel(p, sources, n, dev, split=-1):
+        return {1: recv_1, 2: recv_2, 3: recv_3, 4: recv_4}[p].at[{1: u // 2, 3: max(u - FIRST + 1, 0)}.get(p, u)]
+
+    def to_panel(p, sources, dev, split=-1):
         copies = []
         for u, src in enumerate(sources):
             dst = unit(p, u)
             if u == split:
                 for t in range(per_row):
-                    sem = halves.at[t] if p == SHIFTS else landed(p, u)
-                    copies.append(remote(src.at[t], dst.at[t], send_a.at[n], sem, dev))
+                    sem = landed(p, units - 1 + t if p == SHIFTS and t else u)
+                    copies.append(remote(src.at[t], dst.at[t], send_a, sem, dev))
             else:
-                copies.append(remote(src, dst, send_a.at[n], landed(p, u), dev))
+                copies.append(remote(src, dst, send_a, landed(p, u), dev))
         return copies
 
     def panel(p):
         return [unit(p, u) for u in range(units)]
 
     swap = [
-        remote(a_ref.at[(1 - dep) * half + r], unit(0, half + r), send_a.at[0], recv_a.at[(SHIFTS - 1) * units + half + r // 2], twin_dev)
+        remote(a_ref.at[(1 - dep) * half + r], unit(0, half + r), send_a, swapped, twin_dev)
         for r in range(half)
     ]
-    chain = to_panel(2, own, 0, down)
-    chain2 = to_panel(4, panel(2), 1, down, SPLIT)
-    skip = to_panel(4, own, 1, down2, SPLIT)
-    own_x1 = to_panel(1, own, 0, side_dev)
-    fwd_x1 = to_panel(1, panel(2), 0, side_dev)
-    fwd_x3 = to_panel(3, panel(2), 2, side_dev)
-    top_x3 = to_panel(3, panel(4)[: units - LATE], 2, side_dev, SPLIT)
-    low_x3 = to_panel(3, panel(1), 2, down)
-
-    near_b = [remote(b_ref.at[m_near[k]], near_twin[k], send_b, passed.at[2], twin_dev) for k in range(2)]
+    chain = to_panel(2, own, down)
+    chain2 = to_panel(4, panel(2), down, SPLIT)
+    skip = to_panel(4, own, down2, SPLIT)
+    own_x1 = to_panel(1, own, side_dev)
+    fwd_x1 = to_panel(1, panel(2), side_dev)
+    fwd_x3 = to_panel(3, panel(2), side_dev)
+    top_x3 = to_panel(3, panel(4)[: units - LATE], side_dev, SPLIT)
+    low_x3 = to_panel(3, panel(1), down)
+
+    near_b = [remote(b_ref.at[m_near[k]], near_twin[k], send_b, passed.at[0], twin_dev) for k in range(2)]
     far_b, pass_b = [], []
     for k, sizes in enumerate(PARTS):
         for c, blocks in enumerate(sizes):
@@ -285,16 +287,16 @@
             )
             pass_b.append(remote(far_own[k].at[part], far_twin[k].at[part], send_b, passed.at[k], twin_dev))
 
-    def index_a(src, dst, n, sem, dev):
-        return remote(MA.at[pl.ds(src, n)], MA.at[pl.ds(dst, n)], send_m.at[sem], recv_m.at[min(dst // 2, 3)], dev)
+    def index_a(src, dst, dev):
+        return remote(MA.at[pl.ds(src, 2)], MA.at[pl.ds(dst, 2)], send_m.at[0], recv_m.at[min(dst // 2, 3)], dev)
 
     swap_m = remote(MA.at[0], MA.at[1], send_m.at[0], recv_m.at[0], twin_dev)
     near_m = remote(MB.at[0], MB.at[1], send_m.at[1], recv_m.at[4], twin_dev)
     far_m = remote(MB.at[0], MB.at[2], send_m.at[1], recv_m.at[5], row_dev)
     pass_m = remote(MB.at[2], MB.at[3], send_m.at[1], recv_m.at[4], twin_dev)
-    chain_m, chain2_m, skip_m = index_a(0, 4, 2, 0, down), index_a(4, 8, 2, 2, down), index_a(0, 8, 2, 3, down2)
-    own_x1_m, fwd_x1_m = index_a(0, 2, 2, 0, side_dev), index_a(4, 2, 2, 0, side_dev)
-    fwd_x3_m, low_x3_m = index_a(4, 6, 2, 4, side_dev), index_a(2, 6, 2, 4, down)
+    chain_m, chain2_m, skip_m = index_a(0, 4, down), index_a(4, 8, down), index_a(0, 8, down2)
+    own_x1_m, fwd_x1_m = index_a(0, 2, side_dev), index_a(4, 2, side_dev)
+    fwd_x3_m, low_x3_m = index_a(4, 6, side_dev), index_a(2, 6, down)
 
     drain(MA.at[0], local_sem.at[0])
     drain(MB.at[0], local_sem.at[1])
@@ -306,8 +308,7 @@
     swap_m.wait_recv()
     start([chain_m] + chain[2:half], z > 0)
     start([own_x1_m] + own_x1[2:half], side1)
-    for n in range(half // 2):
-        drain(A.at[pl.ds(0, 2)], recv_a.at[(SHIFTS - 1) * units + half + n])
+    drain(A.at[pl.ds(0, half)], swapped)
 
     @pl.when(z == 0)
     def _():
@@ -334,9 +335,14 @@
     def recv(p, u):
         if p == 4 and u == SPLIT:
             for t in range(per_row):
-                drain(unit(p, u).at[t], halves.at[t])
-        else:
+                recv_half(t)
+        elif p != 3 or u >= FIRST:
             drain(unit(p, u), landed(p, u))
+        elif u == 0:
+            drain(A.at[pl.ds(0, FIRST)], landed(p, u))
+
+    def recv_half(t):
+        drain(unit(SHIFTS, SPLIT).at[t], landed(SHIFTS, units - 1 + t if t else SPLIT))
 
     groups = [(s, m, k, d, far) for k in range(2) for far, s, m in ((0, s_near[k], m_near[k]), (1, s_far[k], m_mine[k]))
               for d in range(2)]
@@ -366,18 +372,26 @@
 
     rights = (Bn0, Gn0, Bf0, Gf0, Bn1, Gn1, Bf1, Gf1)
 
+    def dots(g, r):
+        s, _, _, d, _ = groups[g]
+        values = []
+        for t in range(per_row):
+            here = r * terms + g * per_row + t
+            left = A[(s + row) * units + d * half + r, t]
+            values.append((here, jnp.dot(left, rights[g][ktab[here]], preferred_element_type=jnp.float32)))
+        return values
+
+    def add(values):
+        for here, value in values:
+            run[here] = value + run[ptab[here]]
+
     def products(wanted):
-        held = None
+        held = []
         for g, r in wanted:
-            s, _, _, d, _ = groups[g]
-            for t in range(per_row):
-                here = r * terms + g * per_row + t
-                left = A[(s + row) * units + d * half + r, t]
-                value = jnp.dot(left, rights[g][ktab[here]], preferred_element_type=jnp.float32)
-                if held is not None:
-                    run[held[0]] = held[1] + run[ptab[held[0]]]
-                held = here, value
-        run[held[0]] = held[1] + run[ptab[held[0]]]
+            fresh = dots(g, r)
+            add(held)
+            held = fresh
+        add(held)
 
     def whole_group(g):
         products([(g, r) for r in range(half)])
@@ -404,10 +418,10 @@
             pass_m.start()
         if u in (4, 6):
             low(u - 4)
-        if u in (3, 7):
-            far_part(u // 4)
-
-    def near_units(*wanted):
+        if u == units - 1:
+            far_part(0)
+
+    def arrive_near(*wanted):
         @pl.when(row != side)
         def _():
             for u in wanted:
@@ -418,9 +432,11 @@
             for u in wanted:
                 recv(4, u)
 
+    def near_units(*wanted):
+        arrive_near(*wanted)
         products([(4 + u // half, u % half) for u in wanted])
 
-    def far_units(*wanted):
+    def arrive_far(*wanted):
         @pl.when(row == side)
         def _():
             for u in wanted:
@@ -428,9 +444,12 @@
 
         if units - 1 in wanted:
             pl.when(both(row1, side0))(lambda: recv(4, units - 1))
+
+    def far_units(*wanted):
+        arrive_far(*wanted)
         products([(6 + u // half, u % half) for u in wanted])
 
-    scalars = [pltpu.make_async_copy(MA, SA, local_sem.at[0]), pltpu.make_async_copy(MB, SB, local_sem.at[1])]
+    scalars = [pltpu.make_async_copy(MA.at[pl.ds(0, 2 * REACH)], SA, local_sem.at[0]), pltpu.make_async_copy(MB, SB, local_sem.at[1])]
 
     for u in range(units):
         if u < units - LATE:
@@ -438,7 +457,7 @@
             def _():
                 if u == SPLIT:
                     for t in range(per_row):
-                        drain(unit(4, u).at[t], halves.at[t])
+                        recv_half(t)
                         top_x3[u + t].start()
                 else:
                     recv(4, u)
@@ -455,10 +474,9 @@
             for copy in scalars:
                 copy.wait()
             drain(A.at[pl.ds(0, 2 * units + half)], local_sem.at[2])
-            drain(A.at[pl.ds(0, 2 * units)], passed.at[2])
-            drain(A.at[pl.ds(0, units)], passed.at[0])
+            drain(A.at[pl.ds(0, 3 * units)], passed.at[0])
         if u in (3, 5):
-            far_part((u + 1) // 2)
+            far_part(u // 2)
         if u in (1, 2):
             for r in range((u - 1) * half // 2, u * half // 2):
                 tables(r)
@@ -474,12 +492,29 @@
             near_units(1, 2)
     far_part(len(far_b) - 1)
 
-    def place(*rows):
-        for r in rows:
-            for c in range(out_cols):
-                out_ref[r * size : (r + 1) * size, c * size : (c + 1) * size] = run[ltab[r * out_cols + c]].astype(
-                    out_ref.dtype
-                )
+    def place(r):
+        for c in range(out_cols):
+            out_ref[r * size : (r + 1) * size, c * size : (c + 1) * size] = run[ltab[r * out_cols + c]].astype(
+                out_ref.dtype
+            )
+
+    def finish(*rows, near=False):
+        wanted = [half + r for r in rows]
+        if near:
+            arrive_near(units - 1)
+            wanted.append(half - 1)
+        arrive_far(*wanted)
+        steps = [(7, r) for r in rows]
+        if near:
+            steps[-1:] = [(5, half - 1), (6, half - 1), (7, half - 1)]
+        held = None
+        for g, r in steps + [(None, None)]:
+            fresh = None if g is None else (g, r, dots(g, r))
+            if held is not None:
+                add(held[2])
+                if held[0] == 7:
+                    place(held[1])
+            held = fresh
 
     def last_pass():
         drain(A.at[pl.ds(0, units)], passed.at[1])
@@ -489,18 +524,15 @@
         near_units(3, 4, 5, 6, 7)
         far_units(0, 1, 2, 3)
         last_pass()
-        far_units(4, 5, 6, 7)
-        place(0, 1, 2, 3)
+        finish(0, 1, 2, 3)
 
     @pl.when(both(side1, z < top))
     def _():
         near_units(3, 4, 5, 6, 7)
         far_units(0, 1, 2, 3)
         last_pass()
-        far_units(4, 5)
-        place(0, 1)
-        far_units(6, 7)
-        place(2, 3)
+        finish(0, 1)
+        finish(2, 3)
 
     @pl.when(both(side1, z == top))
     def _():
@@ -511,31 +543,19 @@
         last_pass()
         near_units(6)
         far_units(2)
-        far_units(4, 5)
-        place(0, 1)
-        near_units(7)
-        far_units(3)
-        far_units(6, 7)
-        place(2, 3)
-
-    def sent(n, sem, *flags):
-        if flags:
-            pl.when(both(*flags))(lambda: drain(A.at[pl.ds(0, n)], sem))
-        else:
-            drain(A.at[pl.ds(0, n)], sem)
-
-    sent(2 * units + half, send_a.at[0])
-    sent(units, send_a.at[1], row1, z > 1)
-    sent(2 * units, send_a.at[1], row1, z == 1)
-    sent(2 * units, send_a.at[2], side1, row0)
-    sent(units + LATE, send_a.at[2], side1, row1)
-    sent(units - LATE, send_a.at[2], side0, row1)
+        finish(0, 1)
+        finish(2, 3, near=True)
+
+    for r in range(2):
+        for side_n, flag in enumerate((side0, side1)):
+            for more, where in (((0, z >= 0),) if r == 0 else ((0, z == 0), (2, z == 1), (1, z > 1))):
+                here = both(row == r, flag, where)
+                across = (0, 2 * units) if r == 0 else (units - LATE, units + LATE)
+                n = 2 * units + half + across[side_n] + more * units
+                pl.when(here)(functools.partial(drain, run.at[pl.ds(0, n)], send_a))
+                pl.when(here)(functools.partial(drain, MA.at[pl.ds(0, 5 + 4 * side_n + 2 * more)], send_m.at[0]))
     drain(run.at[pl.ds(0, 6 * units)], send_b)
-    drain(MA.at[pl.ds(0, 5)], send_m.at[0])
     drain(MB.at[pl.ds(0, 3)], send_m.at[1])
-    pl.when(both(row1, z > 0))(lambda: drain(MA.at[pl.ds(0, 2)], send_m.at[2]))
-    pl.when(both(row1, z == 1))(lambda: drain(MA.at[pl.ds(0, 2)], send_m.at[3]))
-    pl.when(side1)(lambda: drain(MA.at[pl.ds(0, 4)], send_m.at[4]))
 
 
 def local_fast(n_col, a_tiles, a_cols, a_count, b_tiles, b_cols, b_count):
@@ -545,6 +565,7 @@
     count = half * SHIFTS * 2 * per_row
     hbm = pl.BlockSpec(memory_space=pltpu.HBM)
     index_shapes = [(REACH * 2, per_row + 1, block_rows), (4, 2, slots, 1, inner)]
+    index_vmem = [(REACH * 2 + 4, per_row + 1, block_rows), index_shapes[1]]
     call = pl.pallas_call(
         functools.partial(gather_multiply, n_col),
         out_shape=jax.ShapeDtypeStruct((half * size, BC * size), jnp.bfloat16),
@@ -552,21 +573,24 @@
         out_specs=pl.BlockSpec(memory_space=pltpu.VMEM),
         scratch_shapes=[pltpu.VMEM((REACH * block_rows, per_row, size, size), jnp.bfloat16)]
         + [pltpu.VMEM((inner, size, size), jnp.bfloat16)] * 8
-        + [pltpu.VMEM(shape, jnp.int32) for shape in index_shapes]
+        + [pltpu.VMEM(shape, jnp.int32) for shape in index_vmem]
         + [pltpu.SMEM(shape, jnp.int32) for shape in index_shapes]
         + [
             pltpu.VMEM((count + 1, size, size), jnp.float32),
             pltpu.SMEM((count,), jnp.int32),
             pltpu.SMEM((count,), jnp.int32),
             pltpu.SMEM((half * BC,), jnp.int32),
-            pltpu.SemaphoreType.DMA((5,)),
+            pltpu.SemaphoreType.DMA((2,)),
             pltpu.SemaphoreType.DMA((6,)),
-            pltpu.SemaphoreType.DMA((3,)),
-            pltpu.SemaphoreType.DMA(((SHIFTS - 1) * block_rows + half + half // 2,)),
+            pltpu.SemaphoreType.DMA,
+            pltpu.SemaphoreType.DMA((half,)),
+            pltpu.SemaphoreType.DMA((block_rows,)),
+            pltpu.SemaphoreType.DMA((block_rows - FIRST + 1,)),
+            pltpu.SemaphoreType.DMA((block_rows + 1,)),
+            pltpu.SemaphoreType.DMA,
             pltpu.SemaphoreType.DMA,
             pltpu.SemaphoreType.DMA((sum(map(len, PARTS)),)),
-            pltpu.SemaphoreType.DMA((3,)),
-            pltpu.SemaphoreType.DMA((per_row,)),
+            pltpu.SemaphoreType.DMA((2,)),
             pltpu.SemaphoreType.REGULAR((3,)),
             pltpu.SemaphoreType.DMA((3,)),
         ],

time: 31.4 us -> 31.4 us (level)
  no operation moved by 1% of the time
where the time goes in v6:
time: 31.4 us; the launch traced here: 31.2 us
  Pallas kernels  30.1 us (96%)
  local copies, waits for them, and re-layouts  1.15 us (4%)
    pallas_call x1, Pallas kernels, local_fast(): call(*(pltpu.with_memory_space_constraint(x, pltpu.HBM) for x in operands))  30.1 us
    unnamed x1, local copies, waits for them, and re-layouts  1.15 us

profile of v6, /device:TPU:30, one launch (start us, length us, event | category | flops | bytes accessed | tf_op | source)
XLA Modules:
  0.0 31.2 jit_solution(10537431336494692594)
XLA Ops:
  0.0 30.1 %shard_map.64 = bf16[512,1536]{1,0:T(8,128)(2,1)S(1)} custom-call(s32[2,8]{1,0:T(2,128)} %bitcast.16, s32[1,8]{1,0:T(1,128)} %bitcast.17, s32[4,1,16]{2,1,0:T(1,128)} %bitcast.14, s32[4,1,16]{2,1,0:T(1,128)} %bitcast.15, bf16[8,2,128,128]{3,2,1,0:T(8,128)(2,1)} %bitcast.13, bf16[4,16,128,128]{3,2,1,0:T(8,128)(2,1)} %bitcast.12), custom_call_target="tpu_custom_call" | custom-call | tf_op jit(solution)/shard_map/pallas_call | solution.py:609
  30.1 1.1 %copy.10 = bf16[512,1536]{1,0:T(8,128)(2,1)} copy(bf16[512,1536]{1,0:T(8,128)(2,1)S(1)} %shard_map.64) | data formatting | bytes 3145728

commit v7 on v6

--- a/solution.py
+++ b/solution.py
@@ -236,10 +236,10 @@
     pl.when(both(row1, z == 1))(lambda: signal(barrier, down2))
     greeted = 1 + row + side + jnp.where(z > 0, 1, 0) + jnp.where(z == top, 1 + row, 0)
     pl.semaphore_wait(barrier, greeted)
+    pl.when(z == top)(lambda: signal(ready.at[2], up))
+    pl.when(both(row1, z == top))(lambda: signal(ready.at[2], up2))
     pl.when(row1)(lambda: signal(ready.at[0], row_dev))
     pl.when(side1)(lambda: signal(ready.at[1], side_dev))
-    pl.when(z == top)(lambda: signal(ready.at[2], up))
-    pl.when(both(row1, z == top))(lambda: signal(ready.at[2], up2))
 
     def unit(p, u):
         return A.at[p * units + u]
@@ -270,7 +270,8 @@
     ]
     chain = to_panel(2, own, down)
     chain2 = to_panel(4, panel(2), down, SPLIT)
-    skip = to_panel(4, own, down2, SPLIT)
+    skip = to_panel(4, panel(0), down2, SPLIT)
+    wrap = to_panel(2, panel(0)[:half], down)
     own_x1 = to_panel(1, own, side_dev)
     fwd_x1 = to_panel(1, panel(2), side_dev)
     fwd_x3 = to_panel(3, panel(2), side_dev)
@@ -310,13 +311,18 @@
     start([own_x1_m] + own_x1[2:half], side1)
     drain(A.at[pl.ds(0, half)], swapped)
 
+    def local_data():
+        drain(A.at[pl.ds(0, 2 * units + half)], local_sem.at[2])
+
     @pl.when(z == 0)
     def _():
+        local_data()
         pl.semaphore_wait(ready.at[2], 1)
-        start([chain_m] + chain[:half])
+        start([chain_m] + wrap)
 
     @pl.when(both(row1, z == 1))
     def _():
+        local_data()
         pl.semaphore_wait(ready.at[2], 1)
         start([skip_m] + skip)
 
@@ -473,7 +479,7 @@
         if u == 1:
             for copy in scalars:
                 copy.wait()
-            drain(A.at[pl.ds(0, 2 * units + half)], local_sem.at[2])
+            pl.when(z > row)(local_data)
             drain(A.at[pl.ds(0, 3 * units)], passed.at[0])
         if u in (3, 5):
             far_part(u // 2)
@@ -532,7 +538,8 @@
         far_units(0, 1, 2, 3)
         last_pass()
         finish(0, 1)
-        finish(2, 3)
+        finish(3)
+        finish(2)
 
     @pl.when(both(side1, z == top))
     def _():
@@ -544,7 +551,8 @@
         near_units(6)
         far_units(2)
         finish(0, 1)
-        finish(2, 3, near=True)
+        finish(3, near=True)
+        finish(2)
 
     for r in range(2):
         for side_n, flag in enumerate((side0, side1)):

time: 31.4 us -> 31.2 us (level)
  no operation moved by 1% of the time
where the time goes in v7:
time: 31.2 us; the launch traced here: 31.1 us
  Pallas kernels  29.9 us (96%)
  local copies, waits for them, and re-layouts  1.15 us (4%)
    pallas_call x1, Pallas kernels, local_fast(): call(*(pltpu.with_memory_space_constraint(x, pltpu.HBM) for x in operands))  29.9 us
    unnamed x1, local copies, waits for them, and re-layouts  1.15 us

profile of v7, /device:TPU:30, one launch (start us, length us, event | category | flops | bytes accessed | tf_op | source)
XLA Modules:
  0.0 31.1 jit_solution(14007993429708535880)
XLA Ops:
  0.0 29.9 %shard_map.64 = bf16[512,1536]{1,0:T(8,128)(2,1)S(1)} custom-call(s32[2,8]{1,0:T(2,128)} %bitcast.16, s32[1,8]{1,0:T(1,128)} %bitcast.17, s32[4,1,16]{2,1,0:T(1,128)} %bitcast.14, s32[4,1,16]{2,1,0:T(1,128)} %bitcast.15, bf16[8,2,128,128]{3,2,1,0:T(8,128)(2,1)} %bitcast.13, bf16[4,16,128,128]{3,2,1,0:T(8,128)(2,1)} %bitcast.12), custom_call_target="tpu_custom_call" | custom-call | tf_op jit(solution)/shard_map/pallas_call | solution.py:617
  29.9 1.1 %copy.10 = bf16[512,1536]{1,0:T(8,128)(2,1)} copy(bf16[512,1536]{1,0:T(8,128)(2,1)S(1)} %shard_map.64) | data formatting | bytes 3145728

commit v8 on v7

--- a/solution.py
+++ b/solution.py
@@ -145,6 +145,7 @@
 PARTS = ((16,), (7, 6, 3))
 LATE = 1
 SPLIT = 6
+PIECES = ((0, 0, 2), (1, 0, 1), (1, 1, 1))
 FIRST = 3
 MESH_ID = pl.DeviceIdType.MESH
 
@@ -249,14 +250,18 @@
     def landed(p, u):
         return {1: recv_1, 2: recv_2, 3: recv_3, 4: recv_4}[p].at[{1: u // 2, 3: max(u - FIRST + 1, 0)}.get(p, u)]
 
+    def piece(ref, n):
+        t, begin, length = PIECES[n]
+        return ref.at[t, pl.ds(begin * size // 2, length * size // 2)]
+
     def to_panel(p, sources, dev, split=-1):
         copies = []
         for u, src in enumerate(sources):
             dst = unit(p, u)
             if u == split:
-                for t in range(per_row):
-                    sem = landed(p, units - 1 + t if p == SHIFTS and t else u)
-                    copies.append(remote(src.at[t], dst.at[t], send_a, sem, dev))
+                for n in range(len(PIECES)):
+                    sem = landed(p, units - 1 + n if p == SHIFTS and n else u)
+                    copies.append(remote(piece(src, n), piece(dst, n), send_a, sem, dev))
             else:
                 copies.append(remote(src, dst, send_a, landed(p, u), dev))
         return copies
@@ -340,15 +345,15 @@
 
     def recv(p, u):
         if p == 4 and u == SPLIT:
-            for t in range(per_row):
-                recv_half(t)
+            for n in range(len(PIECES)):
+                recv_piece(n)
         elif p != 3 or u >= FIRST:
             drain(unit(p, u), landed(p, u))
         elif u == 0:
             drain(A.at[pl.ds(0, FIRST)], landed(p, u))
 
-    def recv_half(t):
-        drain(unit(SHIFTS, SPLIT).at[t], landed(SHIFTS, units - 1 + t if t else SPLIT))
+    def recv_piece(n):
+        drain(piece(unit(SHIFTS, SPLIT), n), landed(SHIFTS, units - 1 + n if n else SPLIT))
 
     groups = [(s, m, k, d, far) for k in range(2) for far, s, m in ((0, s_near[k], m_near[k]), (1, s_far[k], m_mine[k]))
               for d in range(2)]
@@ -417,7 +422,7 @@
             start([chain[half + u]])
             start([own_x1[half + u]], side1)
         else:
-            start(chain2[2 * (u - half) : 2 * (u - half) + 2 + (u == units - 1)], row1, z > 0)
+            start(chain2[2 * (u - half) : 2 * (u - half) + 2 + (u // (units - 1)) * (len(PIECES) - 1)], row1, z > 0)
             start(fwd_x3[2 * (u - half) : 2 * (u - half) + 2], side1)
         if u == 0:
             far_m.wait_recv()
@@ -462,9 +467,9 @@
             @pl.when(both(row1, side0))
             def _():
                 if u == SPLIT:
-                    for t in range(per_row):
-                        recv_half(t)
-                        top_x3[u + t].start()
+                    for n in range(len(PIECES)):
+                        recv_piece(n)
+                        top_x3[u + n].start()
                 else:
                     recv(4, u)
                     top_x3[u].start()
@@ -594,7 +599,7 @@
             pltpu.SemaphoreType.DMA((half,)),
             pltpu.SemaphoreType.DMA((block_rows,)),
             pltpu.SemaphoreType.DMA((block_rows - FIRST + 1,)),
-            pltpu.SemaphoreType.DMA((block_rows + 1,)),
+            pltpu.SemaphoreType.DMA((block_rows + len(PIECES) - 1,)),
             pltpu.SemaphoreType.DMA,
             pltpu.SemaphoreType.DMA,
             pltpu.SemaphoreType.DMA((sum(map(len, PARTS)),)),

time: 31.2 us -> 31.2 us (level)
  no operation moved by 1% of the time
where the time goes in v8:
time: 31.2 us; the launch traced here: 31.1 us
  Pallas kernels  29.9 us (96%)
  local copies, waits for them, and re-layouts  1.15 us (4%)
    pallas_call x1, Pallas kernels, local_fast(): call(*(pltpu.with_memory_space_constraint(x, pltpu.HBM) for x in operands))  29.9 us
    unnamed x1, local copies, waits for them, and re-layouts  1.15 us

profile of v8, /device:TPU:30, one launch (start us, length us, event | category | flops | bytes accessed | tf_op | source)
XLA Modules:
  0.0 31.1 jit_solution(15793432685569645525)
XLA Ops:
  0.0 29.9 %shard_map.64 = bf16[512,1536]{1,0:T(8,128)(2,1)S(1)} custom-call(s32[2,8]{1,0:T(2,128)} %bitcast.16, s32[1,8]{1,0:T(1,128)} %bitcast.17, s32[4,1,16]{2,1,0:T(1,128)} %bitcast.14, s32[4,1,16]{2,1,0:T(1,128)} %bitcast.15, bf16[8,2,128,128]{3,2,1,0:T(8,128)(2,1)} %bitcast.13, bf16[4,16,128,128]{3,2,1,0:T(8,128)(2,1)} %bitcast.12), custom_call_target="tpu_custom_call" | custom-call | tf_op jit(solution)/shard_map/pallas_call | solution.py:622
  29.9 1.1 %copy.10 = bf16[512,1536]{1,0:T(8,128)(2,1)} copy(bf16[512,1536]{1,0:T(8,128)(2,1)S(1)} %shard_map.64) | data formatting | bytes 3145728

commit v9 on v8

--- a/solution.py
+++ b/solution.py
@@ -409,12 +409,12 @@
 
     for u in range(units):
         recv(2, u)
+        start([fwd_x1[u]], side0)
         if u == 0:
             drain(MA.at[pl.ds(4, 2)], recv_m.at[2])
             start([chain2_m], row1, z > 0)
             start([fwd_x1_m], side0)
             start([fwd_x3_m], side1)
-        start([fwd_x1[u]], side0)
         if u == 2:
             drain(MA.at[pl.ds(2, 2)], recv_m.at[1])
             start([low_x3_m], side1)

time: 31.2 us -> 31.2 us (level)
  no operation moved by 1% of the time
where the time goes in v9:
time: 31.2 us; the launch traced here: 31.1 us
  Pallas kernels  29.9 us (96%)
  local copies, waits for them, and re-layouts  1.15 us (4%)
    pallas_call x1, Pallas kernels, local_fast(): call(*(pltpu.with_memory_space_constraint(x, pltpu.HBM) for x in operands))  29.9 us
    unnamed x1, local copies, waits for them, and re-layouts  1.15 us

profile of v9, /device:TPU:30, one launch (start us, length us, event | category | flops | bytes accessed | tf_op | source)
XLA Modules:
  0.0 31.1 jit_solution(278166166558561508)
XLA Ops:
  0.0 29.9 %shard_map.64 = bf16[512,1536]{1,0:T(8,128)(2,1)S(1)} custom-call(s32[2,8]{1,0:T(2,128)} %bitcast.16, s32[1,8]{1,0:T(1,128)} %bitcast.17, s32[4,1,16]{2,1,0:T(1,128)} %bitcast.14, s32[4,1,16]{2,1,0:T(1,128)} %bitcast.15, bf16[8,2,128,128]{3,2,1,0:T(8,128)(2,1)} %bitcast.13, bf16[4,16,128,128]{3,2,1,0:T(8,128)(2,1)} %bitcast.12), custom_call_target="tpu_custom_call" | custom-call | tf_op jit(solution)/shard_map/pallas_call | solution.py:622
  29.9 1.1 %copy.10 = bf16[512,1536]{1,0:T(8,128)(2,1)} copy(bf16[512,1536]{1,0:T(8,128)(2,1)S(1)} %shard_map.64) | data formatting | bytes 3145728

commit v10 on v9

--- a/solution.py
+++ b/solution.py
@@ -323,13 +323,13 @@
     def _():
         local_data()
         pl.semaphore_wait(ready.at[2], 1)
-        start([chain_m] + wrap)
+        start(wrap[:1] + [chain_m] + wrap[1:])
 
     @pl.when(both(row1, z == 1))
     def _():
         local_data()
         pl.semaphore_wait(ready.at[2], 1)
-        start([skip_m] + skip)
+        start(skip[:1] + [skip_m] + skip[1:])
 
     pl.when(side0)(lambda: pl.semaphore_wait(ready.at[1], 1))
     run[zero_at] = jnp.zeros(run.shape[1:], jnp.float32)
@@ -527,6 +527,19 @@
                     place(held[1])
             held = fresh
 
+    def all_sent(side_n):
+        cases = [(0, 2 * units * side_n, row0)]
+        across = units + LATE if side_n else units - LATE
+        cases += [(more, across, both(row1, flag)) for more, flag in ((0, z == 0), (2, z == 1), (1, z > 1))]
+        for more, extra, here in cases:
+            def left(more=more, extra=extra):
+                drain(run.at[pl.ds(0, 2 * units + half + extra + more * units)], send_a)
+                drain(MA.at[pl.ds(0, 5 + 4 * side_n + 2 * more)], send_m.at[0])
+
+            pl.when(here)(left)
+        drain(run.at[pl.ds(0, 6 * units)], send_b)
+        drain(MB.at[pl.ds(0, 3)], send_m.at[1])
+
     def last_pass():
         drain(A.at[pl.ds(0, units)], passed.at[1])
 
@@ -536,6 +549,7 @@
         far_units(0, 1, 2, 3)
         last_pass()
         finish(0, 1, 2, 3)
+        all_sent(0)
 
     @pl.when(both(side1, z < top))
     def _():
@@ -544,6 +558,7 @@
         last_pass()
         finish(0, 1)
         finish(3)
+        all_sent(1)
         finish(2)
 
     @pl.when(both(side1, z == top))
@@ -556,19 +571,9 @@
         near_units(6)
         far_units(2)
         finish(0, 1)
+        all_sent(1)
         finish(3, near=True)
         finish(2)
-
-    for r in range(2):
-        for side_n, flag in enumerate((side0, side1)):
-            for more, where in (((0, z >= 0),) if r == 0 else ((0, z == 0), (2, z == 1), (1, z > 1))):
-                here = both(row == r, flag, where)
-                across = (0, 2 * units) if r == 0 else (units - LATE, units + LATE)
-                n = 2 * units + half + across[side_n] + more * units
-                pl.when(here)(functools.partial(drain, run.at[pl.ds(0, n)], send_a))
-                pl.when(here)(functools.partial(drain, MA.at[pl.ds(0, 5 + 4 * side_n + 2 * more)], send_m.at[0]))
-    drain(run.at[pl.ds(0, 6 * units)], send_b)
-    drain(MB.at[pl.ds(0, 3)], send_m.at[1])
 
 
 def local_fast(n_col, a_tiles, a_cols, a_count, b_tiles, b_cols, b_count):

time: 31.2 us -> 31.2 us (level)
  no operation moved by 1% of the time
where the time goes in v10:
time: 31.2 us; the launch traced here: 31 us
  Pallas kernels  29.8 us (96%)
  local copies, waits for them, and re-layouts  1.15 us (4%)
    pallas_call x1, Pallas kernels, local_fast(): call(*(pltpu.with_memory_space_constraint(x, pltpu.HBM) for x in operands))  29.8 us
    unnamed x1, local copies, waits for them, and re-layouts  1.15 us

profile of v10, /device:TPU:30, one launch (start us, length us, event | category | flops | bytes accessed | tf_op | source)
XLA Modules:
  0.0 31.0 jit_solution(11353894286761164074)
XLA Ops:
  0.0 29.8 %shard_map.64 = bf16[512,1536]{1,0:T(8,128)(2,1)S(1)} custom-call(s32[2,8]{1,0:T(2,128)} %bitcast.16, s32[1,8]{1,0:T(1,128)} %bitcast.17, s32[4,1,16]{2,1,0:T(1,128)} %bitcast.14, s32[4,1,16]{2,1,0:T(1,128)} %bitcast.15, bf16[8,2,128,128]{3,2,1,0:T(8,128)(2,1)} %bitcast.13, bf16[4,16,128,128]{3,2,1,0:T(8,128)(2,1)} %bitcast.12), custom_call_target="tpu_custom_call" | custom-call | tf_op jit(solution)/shard_map/pallas_call | solution.py:627
  29.8 1.1 %copy.10 = bf16[512,1536]{1,0:T(8,128)(2,1)} copy(bf16[512,1536]{1,0:T(8,128)(2,1)S(1)} %shard_map.64) | data formatting | bytes 3145728

commit v11 on v10

--- a/solution.py
+++ b/solution.py
@@ -142,7 +142,7 @@
 
 
 REACH = SHIFTS + 1
-PARTS = ((16,), (7, 6, 3))
+PARTS = ((16,), (8, 6, 2))
 LATE = 1
 SPLIT = 6
 PIECES = ((0, 0, 2), (1, 0, 1), (1, 1, 1))

time: 31.2 us -> 31.2 us (level)
  no operation moved by 1% of the time
where the time goes in v11:
time: 31.2 us; the launch traced here: 31 us
  Pallas kernels  29.8 us (96%)
  local copies, waits for them, and re-layouts  1.15 us (4%)
    pallas_call x1, Pallas kernels, local_fast(): call(*(pltpu.with_memory_space_constraint(x, pltpu.HBM) for x in operands))  29.8 us
    unnamed x1, local copies, waits for them, and re-layouts  1.15 us

profile of v11, /device:TPU:30, one launch (start us, length us, event | category | flops | bytes accessed | tf_op | source)
XLA Modules:
  0.0 31.0 jit_solution(385318934357588900)
XLA Ops:
  0.0 29.8 %shard_map.64 = bf16[512,1536]{1,0:T(8,128)(2,1)S(1)} custom-call(s32[2,8]{1,0:T(2,128)} %bitcast.16, s32[1,8]{1,0:T(1,128)} %bitcast.17, s32[4,1,16]{2,1,0:T(1,128)} %bitcast.14, s32[4,1,16]{2,1,0:T(1,128)} %bitcast.15, bf16[8,2,128,128]{3,2,1,0:T(8,128)(2,1)} %bitcast.13, bf16[4,16,128,128]{3,2,1,0:T(8,128)(2,1)} %bitcast.12), custom_call_target="tpu_custom_call" | custom-call | tf_op jit(solution)/shard_map/pallas_call | solution.py:627
  29.9 1.1 %copy.10 = bf16[512,1536]{1,0:T(8,128)(2,1)} copy(bf16[512,1536]{1,0:T(8,128)(2,1)S(1)} %shard_map.64) | data formatting | bytes 3145728
